TPU v7x, 512 devices: a whole 4x4x16 slice. The times are simulated.
512 devices in a mesh: lat: 16 (over z_hi, y), lon: 32 (over z_lo, x, core).
Axes of the slice: x: 4, y: 4, z: 16 (z_hi: 4, z_lo: 4; z = z_hi * 4 + z_lo), core: 2. Of those that a mesh axis runs over, the one named last changes fastest.
Arguments:
- height: float32 [3072, 12288], P('lat', 'lon'), may hold values from -6 to 6
- flux_lon: float32 [3072, 12288], P('lat', 'lon'), may hold values from -4 to 4
- flux_lat: float32 [3072, 12288], P('lat', 'lon'), may hold values from -4 to 4
- depth: float32 [3072, 12288], P('lat', 'lon'), may hold values from 0.05 to 1
- wet: int32 [3072, 12288], P('lat', 'lon'), may hold values 0 or 1
- kernel: float32 [384, 384, 768], P('lat', None, 'lon'), may hold values from -0.125 to 0.125
Outputs:
- height_out: float32 [3072, 12288], P('lat', 'lon')
- flux_lon_out: float32 [3072, 12288], P('lat', 'lon')
- flux_lat_out: float32 [3072, 12288], P('lat', 'lon')
- loading_out: float32 [384, 768], P('lat', 'lon')
All inputs are finite; a program needn't handle non-finite values. No bound on the sum of `wet` on one device may be relied on, other than what follows from the above.
Results may differ from a plain program's by a relative error of at most 0.00011.
Values sent between devices are 32-bit elements; how exact they have to be, the bound alone decides.
No kernel may reach another device: no remote copies, remote signals or barrier semaphores. Data moves between devices by JAX's collectives and lax.ppermute only.
A program may use at most 128 MiB of HBM per device.

v0:
```python
import math

import jax
import jax.numpy as jnp
from jax import lax
from jax.sharding import PartitionSpec as P

CROWS = 24
CCOLS = 24
STEPS = 2
ROW_RATIO = 8
COL_RATIO = 16


angle_step = math.pi / (180.0 * 240.0)
courant_lon = 0.3
courant_lat = 0.3


def padded(cells, sides, width, closed):
    for axis, dim in sides:
        count = lax.axis_size(axis)
        ends = count if closed else count - 1
        head = lax.slice_in_dim(cells, 0, width, axis=dim)
        tail = lax.slice_in_dim(cells, cells.shape[dim] - width, cells.shape[dim], axis=dim)
        cells = jnp.concatenate(
            [
                lax.ppermute(tail, axis, [(i, (i + 1) % count) for i in range(ends)]),
                cells,
                lax.ppermute(head, axis, [((i + 1) % count, i) for i in range(ends)]),
            ],
            axis=dim,
        )
    return cells


def coslat(position, total):
    return jnp.cos((position - 0.5 * total) * angle_step)


def edge_cols(field):
    return jnp.concatenate([field[:, :1], field[:, -1:]], 1)


def edge_rows(field):
    return jnp.concatenate([field[:1], field[-1:]], 0)


def body(height, flux_lon, flux_lat, depth, wet, kernel):
    lat_count = lax.axis_size("lat")
    lon_count = lax.axis_size("lon")
    rows, cols = height.shape
    grid_rows = rows * lat_count
    mass_rows = kernel.shape[1]
    mass_cols = CCOLS * lon_count
    wetf = wet.astype(jnp.float32)
    global_rows = (lax.axis_index("lat") * rows + jnp.arange(rows, dtype=jnp.int32)).astype(
        jnp.float32
    )
    cos_center = coslat(global_rows + 0.5, grid_rows)[:, None]
    cos_north = coslat(global_rows + 1.0, grid_rows)[:, None]
    cos_south = coslat(global_rows, grid_rows)[:, None]
    offset = lax.axis_index("lon") * CCOLS

    def contract(total, piece, start):
        width = piece.shape[0]
        shifted = jnp.roll(piece, offset, axis=1)
        stacked = jnp.stack([jnp.roll(shifted, lagged, axis=1) for lagged in range(CCOLS)])
        weights = lax.dynamic_slice_in_dim(kernel, start, width, 1)
        return total + jnp.einsum("aje,ejx->ax", weights, stacked, precision=lax.Precision.HIGHEST)

    loading = jnp.zeros((CROWS, CCOLS), jnp.float32)
    for step_index in range(STEPS):
        weighted = height * wetf * cos_center
        mass = weighted.reshape(CROWS, ROW_RATIO, CCOLS, COL_RATIO).mean(axis=(1, 3))
        empty = jnp.zeros((CROWS, mass_cols), jnp.float32)
        everyone = lax.all_gather(mass[None], ("lat", "lon"), axis=0, tiled=True)
        whole = (
            everyone.reshape(lat_count, lon_count, CROWS, CCOLS)
            .transpose(0, 2, 1, 3)
            .reshape(mass_rows, mass_cols)
        )

        def band_term(band, total):
            first = band * CROWS
            return contract(total, lax.dynamic_slice_in_dim(whole, first, CROWS, 0), first)

        partial_sum = lax.fori_loop(0, lat_count, band_term, empty)
        loading = lax.psum_scatter(partial_sum, "lon", scatter_dimension=1, tiled=True)
        zeta = height + jnp.repeat(jnp.repeat(loading, ROW_RATIO, axis=0), COL_RATIO, axis=1)
        lon_edges = jnp.stack(
            [edge_cols(zeta), edge_cols(flux_lon), edge_cols(depth), edge_cols(wetf)]
        )
        lon_rim = padded(lon_edges, (("lon", 2),), 1, True)
        lat_edges = jnp.stack(
            [edge_rows(zeta), edge_rows(flux_lat), edge_rows(depth), edge_rows(wetf)]
        )
        lat_rim = padded(lat_edges, (("lat", 1),), 1, False)
        zeta_lon = jnp.concatenate([lon_rim[0, :, :1], zeta, lon_rim[0, :, 3:]], 1)
        depth_lon = jnp.concatenate([lon_rim[2, :, :1], depth, lon_rim[2, :, 3:]], 1)
        wet_lon = jnp.concatenate([lon_rim[3, :, :1], wetf, lon_rim[3, :, 3:]], 1)
        old_lon = jnp.concatenate([lon_rim[1, :, :1], flux_lon], 1)
        lon_faces = (
            wet_lon[:, :-1]
            * wet_lon[:, 1:]
            * (
                old_lon
                - courant_lon
                / cos_center
                * (0.5 * (depth_lon[:, :-1] + depth_lon[:, 1:]))
                * (zeta_lon[:, 1:] - zeta_lon[:, :-1])
            )
        )
        zeta_lat = jnp.concatenate([lat_rim[0, :1], zeta, lat_rim[0, 3:]], 0)
        depth_lat = jnp.concatenate([lat_rim[2, :1], depth, lat_rim[2, 3:]], 0)
        wet_lat = jnp.concatenate([lat_rim[3, :1], wetf, lat_rim[3, 3:]], 0)
        old_lat = jnp.concatenate([lat_rim[1, :1], flux_lat], 0)
        lat_faces = (
            wet_lat[:-1]
            * wet_lat[1:]
            * (
                old_lat
                - courant_lat
                * (0.5 * (depth_lat[:-1] + depth_lat[1:]))
                * (zeta_lat[1:] - zeta_lat[:-1])
            )
        )
        flux_lon = lon_faces[:, 1:]
        flux_lat = lat_faces[1:]
        height = wetf * (
            height
            - courant_lon / cos_center * (flux_lon - lon_faces[:, :-1])
            - courant_lat / cos_center * (cos_north * flux_lat - cos_south * lat_faces[:-1])
        )
    return (height, flux_lon, flux_lat, loading)


def solution(mesh):
    return jax.shard_map(
        body,
        mesh=mesh,
        in_specs=(
            P("lat", "lon"),
            P("lat", "lon"),
            P("lat", "lon"),
            P("lat", "lon"),
            P("lat", "lon"),
            P("lat", None, "lon"),
        ),
        out_specs=(P("lat", "lon"), P("lat", "lon"), P("lat", "lon"), P("lat", "lon")),
        check_vma=False,
    )
```

profile of v0, /device:TPU:1, one launch (start us, length us, event | category | flops | bytes accessed | tf_op | source)
XLA Modules:
  0.0 2465.6 jit_solution(4905006223194013492)
XLA Ops:
  9.8 2.2 reshape.78
  11.9 2.0 reduce_sum.18
  19.8 817.0 %all-gather.5.cloned.1.call-done = f32[12288,24]{1,0:T(8,128)} async-done(((f32[24,24]{1,0:T(8,128)}), f32[12288,24]{1,0:T(8,128)}) %all-gather.5.cloned.1.call-update) | async-done | bytes 1179664 | tf_op jit(solution)/shard_map/all_gather | solution.py:77
  836.9 6.6 copy.129
  843.4 6.3 reshape.80
  849.7 103.6 %while.28 = (s32[]{:T(128)}, f32[24,768]{1,0:T(8,128)S(1)}, f32[24,384,24]{1,0,2:T(8,128)S(1)}, f32[384,768]{1,0:T(8,128)}, s32[]{:T(128)}, /*index=5*/s32[]{:T(...) while((s32[]{:T(128)}, f32[24,768]{1,0:T(8,128)S(1)}, ...), condition=%wide.region_2.4_spmd.clone, body=%wide.region_1.3_spmd.clone.sunk | while | flops 127881232 | bytes 6307873 | solution.py:88
  893.4 1.7 fusion.177
  899.8 1.7 fusion.177
  906.3 1.7 fusion.177
  912.8 1.7 fusion.177
  919.3 1.7 fusion.177
  954.1 254.3 %all-reduce.5.cloned.1.call-done = f32[24,768]{1,0:T(8,128)} async-done(((f32[24,768]{1,0:T(8,128)}), f32[24,768]{1,0:T(8,128)}) %all-reduce.5.cloned.1.call-update) | async-done | bytes 73744
  1210.2 4.0 collective-permute-start.1
  1214.2 1.9 collective-permute-start
  1218.6 4.0 collective-permute-start.2
  1228.8 2.1 fusion.72
  1233.3 2.2 reshape.83
  1235.5 1.9 reduce_sum.19
  1239.4 824.6 %all-gather.7.cloned.1.call-done = f32[12288,24]{1,0:T(8,128)} async-done(((f32[24,24]{1,0:T(8,128)}), f32[12288,24]{1,0:T(8,128)}) %all-gather.7.cloned.1.call-update) | async-done | bytes 1179664 | tf_op jit(solution)/shard_map/all_gather | solution.py:77
  2063.9 6.6 copy.161
  2070.5 6.3 reshape.85
  2076.8 103.6 %while.29 = (s32[]{:T(128)}, f32[24,768]{1,0:T(8,128)S(1)}, f32[24,384,24]{1,0,2:T(8,128)S(1)}, f32[384,768]{1,0:T(8,128)}, s32[]{:T(128)}, /*index=5*/s32[]{:T(...) while((s32[]{:T(128)}, f32[24,768]{1,0:T(8,128)S(1)}, ...), condition=%wide.region_6.8_spmd.clone, body=%wide.region_5.7_spmd.clone.sunk | while | flops 127881232 | bytes 6307873 | solution.py:88
  2120.4 1.7 fusion.203
  2126.9 1.7 fusion.203
  2133.4 1.7 fusion.203
  2139.9 1.7 fusion.203
  2146.4 1.7 fusion.203
  2181.1 254.4 %all-reduce.7.cloned.1.call-done = f32[24,768]{1,0:T(8,128)} async-done(((f32[24,768]{1,0:T(8,128)}), f32[24,768]{1,0:T(8,128)}) %all-reduce.7.cloned.1.call-update) | async-done | bytes 73744
  2436.6 4.0 collective-permute-start.5
  2440.6 1.9 collective-permute-start.4
  2444.3 4.0 collective-permute-start.6
  2454.2 2.0 fusion.75
  (1694 shorter events, 217.6 us)
Async XLA Ops:
  7.2 829.7 %all-gather.5.cloned.1.call-start = ((), (), s32[]{:S(2)}) async-start(), calls=%async_computation | async-start | bytes 6303744 | tf_op jit(solution)/shard_map/all_gather | solution.py:77
  11.9 2.7 copy-start.5
  11.9 3.7 copy-start.6
  11.9 3.9 copy-start.7
  14.5 1193.9 %all-reduce.5.cloned.1.call-start = ((), (), s32[]{:S(2)}) async-start(), calls=%async_computation.2 | async-start | bytes 147456
  953.4 0.6 copy-start.1
  954.0 1109.9 %all-gather.7.cloned.1.call-start = ((), (), s32[]{:S(2)}) async-start(), calls=%async_computation.1 | async-start | bytes 6303744 | tf_op jit(solution)/shard_map/all_gather | solution.py:77
  1210.2 12.4 collective-permute-start.1
  1214.2 8.5 collective-permute-start
  1217.3 6.5 collective-permute-start.3
  1218.6 5.0 collective-permute-start.2
  1228.8 2.1 copy-start
  1238.0 1197.5 %all-reduce.7.cloned.1.call-start = ((), (), s32[]{:S(2)}) async-start(), calls=%async_computation.3 | async-start | bytes 147456
  2180.4 0.6 copy-start.2
  2180.4 267.9 %copy-start.4 = (f32[192,384]{0,1:T(8,128)S(1)}, f32[192,384]{0,1:T(8,128)}, u32[]{:S(2)}) copy-start(f32[192,384]{0,1:T(8,128)} %get-tuple-element.325) | copy-start | bytes 884740
  2436.3 12.3 copy-start.8
  2436.6 11.7 collective-permute-start.5
  2440.6 7.7 collective-permute-start.4
  2442.8 11.4 copy-start.3
  2442.9 6.3 collective-permute-start.7
  2444.3 4.8 collective-permute-start.6
Sparse Core Ops, SparseCore 0:
  14.7 822.1 all-gather.4
  954.1 254.2 all-reduce.4
  1238.2 825.7 all-gather.6
  2181.2 254.2 all-reduce.6
where the time goes:
time: 2480 us; the launch traced here: 2470 us
  waiting for transfers between devices  2150 us (87%)
  local copies, waits for them, and re-layouts  139 us (6%)
  other arithmetic  76.9 us (3%)
  matrix products  53 us (2%)
    all_gather x2, waiting for transfers between devices, body(): everyone = lax.all_gather(mass[None], ('lat', 'lon'), axis=0, tiled=True)  1640 us
    unnamed x6, waiting for transfers between devices  509 us
    while x736, other arithmetic  61.8 us
    slice x736, local copies, waits for them, and re-layouts, contract(): jnp.roll(shifted, lagged, axis=1)  53.1 us
    dot_general x32, matrix products, contract(): jnp.einsum('aje,ejx->ax', weights, stacked, precision=lax.Precision.HIGHEST)  53 us
  transfers between devices with their start and end apart: 12, of which 5 were waited for; matrix products, arithmetic and copies ran while one was open for 0% of the time, Pallas kernels for 0%

commit v1 on v0

v1 whole, which is shorter than its diff:
```python
import math

import jax
import jax.numpy as jnp
import numpy as np
from jax import lax
from jax.experimental import pallas as pl
from jax.experimental.pallas import tpu as pltpu
from jax.sharding import Mesh
from jax.sharding import PartitionSpec as P

ROWS, COLS = 192, 384
EROWS, ECOLS = 200, 512
GRID_ROWS = 3072
NB = 24
HALO_TILES = 17
STEP_ANGLE = math.pi / (180.0 * 240.0)
COURANT = 0.3
F32 = jnp.float32
BF16 = jnp.bfloat16
HIGHEST = lax.Precision.HIGHEST
VM = pl.BlockSpec(memory_space=pltpu.VMEM)


def iota(shape, dim):
    return lax.broadcasted_iota(jnp.int32, shape, dim)


def cos_row(position):
    angle = (position - 0.5 * GRID_ROWS) * STEP_ANGLE
    s = angle * angle
    return 1.0 + s * (-1.0 / 2 + s * (1.0 / 24 + s * (-1.0 / 720 + s * (1.0 / 40320))))


def lat_index():
    return lax.axis_index("zh") * 4 + lax.axis_index("y")


def mass_tile(weighted):
    pick = (iota((COLS, 128), 0) // 16 == iota((COLS, 128), 1)).astype(F32)
    sums = jnp.dot(weighted, pick, precision=HIGHEST, preferred_element_type=F32)
    sums = jnp.sum(sums.reshape(NB, 8, 128), axis=1) * (1.0 / 128.0)
    tile = sums[0:8]
    for q in range(1, 3):
        tile = tile + pltpu.roll(sums[8 * q : 8 * q + 8], 24 * q, 1)
    return tile


def pack_kernel(h_ref, fl_ref, ft_ref, d_ref, wet_ref, mass_ref, east_ref, west_ref, north_ref, south_ref):
    w = wet_ref[...].astype(F32)
    fields = (h_ref[...], fl_ref[...], ft_ref[...], d_ref[...], w)
    row = (lat_index() * ROWS + iota((ROWS, 128), 0)).astype(F32)
    cosc = jnp.concatenate([cos_row(row + 0.5)] * 3, axis=1)
    tile = mass_tile(fields[0] * w * cosc)
    for z in range(16):
        mass_ref[z] = tile
    lane = iota((ROWS, 128), 1)
    east = jnp.zeros((ROWS, 128), F32)
    west = jnp.zeros((ROWS, 128), F32)
    for f, x in enumerate(fields):
        first, last = x[:, :128], x[:, 256:]
        if f:
            first = pltpu.roll(first, 2 * f, 1)
            last = pltpu.roll(last, 128 - 2 * f, 1)
        west = jnp.where((lane >= 2 * f) & (lane < 2 * f + 2), first, west)
        east = jnp.where((lane >= 126 - 2 * f) & (lane < 128 - 2 * f), last, east)
        for t in range(3):
            at = 8 * (3 * f + t)
            north_ref[at : at + 8, :] = x[ROWS - 8 :, 128 * t : 128 * t + 128]
            south_ref[at : at + 8, :] = x[:8, 128 * t : 128 * t + 128]
    east_ref[...] = east
    west_ref[...] = west


def conv_kernel(mt_ref, k_ref, ks_ref, kn_ref, out_ref, m_ref, s_ref):
    core = lax.axis_index("c")
    lane = iota((8, 128), 1)
    m_ref[...] = jnp.zeros_like(m_ref)
    for yl in range(8):
        zh, y = yl // 4, yl % 4
        for q in range(3):
            parts = [None] * 6
            for b in range(32):
                zl, xc = b // 8, b % 8
                src = mt_ref[y * 8 + xc, zh * 4 + zl]
                t, o = divmod(24 * b, 128)
                shift = (24 * b - 24 * q) % 128
                src = pltpu.roll(src, shift, 1) if shift else src
                parts[t] = jnp.where(lane >= o, src, parts[t]) if o else src
                if o + 24 > 128:
                    parts[t + 1] = src
            rows = jnp.concatenate(parts, axis=1)
            m_ref[pl.ds(pl.multiple_of(core * 64 + (yl * 24 + q * 8), 8), 8), :] = rows
    m = m_ref[...]
    mh = m.astype(BF16)
    ml = (m - mh.astype(F32)).astype(BF16)

    def product(wide):
        wh = wide.astype(BF16)
        wl = (wide - wh.astype(F32)).astype(BF16)
        return (
            jnp.dot(wh, mh, preferred_element_type=F32)
            + jnp.dot(wh, ml, preferred_element_type=F32)
            + jnp.dot(wl, mh, preferred_element_type=F32)
        )

    def lagged(first, second):
        total = pltpu.roll(first, 0, 1, stride=1, stride_axis=0) + pltpu.roll(
            second, 24, 1, stride=1, stride_axis=0
        )
        return jnp.sum(total, axis=0, keepdims=True)

    per = 4
    for group in range(NB // per):
        wide = jnp.concatenate(
            [k_ref[s, per * group : per * group + per].reshape(per * NB, 256) for s in range(2)], axis=0
        )
        p = product(wide)
        for i in range(per):
            a = per * group + i
            s_ref[a + 1 : a + 2, :] = lagged(p[NB * i : NB * i + NB], p[NB * (per + i) : NB * (per + i) + NB])
    wide = jnp.concatenate(
        [jnp.concatenate([r[8 * HALO_TILES : 8 * HALO_TILES + 48], r[8 * HALO_TILES + 48 :]], axis=1) for r in (ks_ref, kn_ref)],
        axis=0,
    )
    p = product(wide)
    s_ref[0:1, :] = lagged(p[0:24], p[24:48])
    s_ref[25:26, :] = lagged(p[48:72], p[72:96])
    s_ref[26:32, :] = jnp.zeros((6, 768), F32)
    base = 2 * (lax.axis_index("zl") * 4 + lax.axis_index("x"))
    for k in range(32):
        start = (24 * k - 1) % 768
        t, o = divmod(start, 128)
        message = jnp.zeros((8, 128), F32)
        for q in range(4):
            shift = (26 * q - start) % 128
            piece = pltpu.roll(s_ref[8 * q : 8 * q + 8, 128 * t : 128 * t + 128], shift, 1)
            held = 128 - o
            if held < 26:
                u = (t + 1) % 6
                other = pltpu.roll(s_ref[8 * q : 8 * q + 8, 128 * u : 128 * u + 128], shift, 1)
                piece = jnp.where(lane >= 26 * q + held, other, piece)
            message = piece if q == 0 else jnp.where(lane >= 26 * q, piece, message)
        out_ref[lax.rem(base + k, 32)] = jnp.where(lane < 104, message, 0.0)


def loading_tile(rs_ref):
    parts = [rs_ref[i] for i in range(32)]
    while len(parts) > 1:
        parts = [parts[i] + parts[i + 1] for i in range(0, len(parts), 2)]
    return parts[0]


def spread(tile):
    lane = iota((8, 128), 1)
    sub = iota((8, 128), 0)
    by_q = []
    for q in range(4):
        cols = []
        for t in range(4):
            j = lane + 128 * t
            v = jnp.where(j < 448, jnp.minimum(j // 16, 24) + 1, 0)
            cols.append(jnp.take_along_axis(tile, v + 26 * q, axis=1))
        by_q.append(cols)

    def coarse(a, t):
        q, s = divmod(a, 8)
        return jnp.broadcast_to(by_q[q][t][s : s + 1, :], (8, 128))

    rows = []
    for i in range(25):
        if i < 24:
            rows.append(jnp.concatenate([coarse(i + 1, t) for t in range(4)], axis=1))
        else:
            rows.append(
                jnp.concatenate([jnp.where(sub < 4, coarse(25, t), coarse(0, t)) for t in range(4)], axis=1)
            )
    return jnp.concatenate(rows, axis=0)


def wide4(x):
    return jnp.concatenate([x] * 4, axis=1)


def fine_step(h, fl, ft, d, w, loading):
    r = iota((EROWS, 128), 0)
    row = (lat_index() * ROWS + jnp.where(r < 196, r, r - EROWS)).astype(F32)
    cosc = cos_row(row + 0.5)
    cosn = wide4(cos_row(row + 1.0))
    coss = wide4(cos_row(row))
    ratio = wide4(COURANT / cosc)

    def east(x):
        return pltpu.roll(x, ECOLS - 1, 1)

    def north(x):
        return pltpu.roll(x, EROWS - 1, 0)

    z = h + loading
    fl = w * east(w) * (fl - ratio * (0.5 * (d + east(d))) * (east(z) - z))
    ft = w * north(w) * (ft - COURANT * (0.5 * (d + north(d))) * (north(z) - z))
    h = w * (
        h - ratio * (fl - pltpu.roll(fl, 1, 1)) - ratio * (cosn * ft - coss * pltpu.roll(ft, 1, 0))
    )
    return h, fl, ft, wide4(cosc)


def first_kernel(
    h_ref, fl_ref, ft_ref, d_ref, wet_ref, fe_ref, fw_ref, fs_ref, fn_ref, rs_ref,
    h_out, fl_out, ft_out, d_out, w_out, mass_ref,
):
    lane = iota((ROWS, 128), 1)
    lane8 = iota((8, 128), 1)
    sub8 = iota((8, 128), 0)

    def side(from_east, from_west, f, at):
        e, w = from_east, from_west
        if f:
            e = pltpu.roll(e, 128 - 2 * f, 1)
            w = pltpu.roll(w, 2 * f, 1)
        return jnp.where(at < 2, e, jnp.where(at >= 126, w, 0.0))

    def edge(ref, f):
        tiles = [ref[8 * (3 * f + t) : 8 * (3 * f + t) + 8, :] for t in range(3)]
        return tiles + [side(ref[120:128, :], ref[128:136, :], f, lane8)]

    ext = []
    for f, x in enumerate((h_ref[...], fl_ref[...], ft_ref[...], d_ref[...], wet_ref[...].astype(F32))):
        main = jnp.concatenate([x, side(fe_ref[...], fw_ref[...], f, lane)], axis=1)
        from_south, from_north = edge(fs_ref, f), edge(fn_ref, f)
        tail = jnp.concatenate(
            [jnp.where(sub8 < 4, n, s) for n, s in zip(from_north, from_south)], axis=1
        )
        ext.append(jnp.concatenate([main, tail], axis=0))
    h, fl, ft, d, w = ext
    h, fl, ft, cosc = fine_step(h, fl, ft, d, w, spread(loading_tile(rs_ref)))
    h_out[...] = h
    fl_out[...] = fl
    ft_out[...] = ft
    d_out[...] = d
    w_out[...] = w
    tile = mass_tile((h * w * cosc)[:ROWS, :COLS])
    for z in range(16):
        mass_ref[z] = tile


def last_kernel(h_ref, fl_ref, ft_ref, d_ref, w_ref, rs_ref, h_out, fl_out, ft_out, load_out):
    tile = loading_tile(rs_ref)
    rows = jnp.concatenate([pltpu.roll(tile, 127 - 26 * q, 1) for q in range(4)], axis=0)
    load_out[...] = pltpu.roll(rows, 31, 0)[:NB, :NB]
    h, fl, ft, _ = fine_step(h_ref[...], fl_ref[...], ft_ref[...], d_ref[...], w_ref[...], spread(tile))
    h_out[...] = h[:ROWS, :COLS]
    fl_out[...] = fl[:ROWS, :COLS]
    ft_out[...] = ft[:ROWS, :COLS]


def struct(*shape):
    return jax.ShapeDtypeStruct(shape, F32)


def call(kernel, name, outs, ins, scratch=()):
    return pl.pallas_call(
        kernel,
        name=name,
        out_shape=outs,
        in_specs=[VM] * len(ins),
        out_specs=jax.tree.map(lambda _: VM, outs),
        scratch_shapes=list(scratch),
    )(*ins)


def body(height, flux_lon, flux_lat, depth, wet, kernel):
    LAT, LON = ("zh", "y"), ("zl", "x", "c")
    fields = (height, flux_lon, flux_lat, depth, wet)
    halves = kernel.transpose(0, 2, 1)
    halves = jnp.stack([halves[:, :, :256], halves[:, :, 128:]])
    mass, to_east, to_west, to_north, to_south = call(
        pack_kernel,
        "pack",
        (struct(16, 8, 128), struct(ROWS, 128), struct(ROWS, 128), struct(120, 128), struct(120, 128)),
        fields,
    )
    up = [(i, (i + 1) % 32) for i in range(32)]
    down = [((i + 1) % 32, i) for i in range(32)]
    from_west = lax.ppermute(to_east, LON, up)
    from_east = lax.ppermute(to_west, LON, down)
    k2 = lax.all_to_all(halves, "c", 0, 0, tiled=True)

    def lat_message(rows, at, edge_row):
        k = k2[:, edge_row].reshape(48, 256)
        return jnp.concatenate(
            [rows, from_east[at : at + 8], from_west[at : at + 8], k[:, :128], k[:, 128:]], axis=0
        )

    from_south = lax.ppermute(lat_message(to_north, ROWS - 8, 23), LAT, [(i, i + 1) for i in range(15)])
    from_north = lax.ppermute(lat_message(to_south, 0, 0), LAT, [(i + 1, i) for i in range(15)])

    def loading_parts(mass):
        column = lax.all_to_all(mass, ("zh", "zl"), 0, 0, tiled=True)
        spreadout = jnp.broadcast_to(column.reshape(1, 2, 64, 128), (16, 2, 64, 128)).reshape(32, 64, 128)
        tiles = lax.all_to_all(spreadout, ("y", "x", "c"), 0, 0, tiled=True)
        partial = call(
            conv_kernel,
            "conv",
            struct(32, 8, 128),
            (tiles.reshape(32, 8, 8, 128), k2, from_south, from_north),
            (pltpu.VMEM((256, 768), F32), pltpu.VMEM((32, 768), F32)),
        )
        return lax.all_to_all(partial, LON, 0, 0, tiled=True)

    parts = loading_parts(mass)
    *state, mass = call(
        first_kernel,
        "first",
        (struct(EROWS, ECOLS),) * 5 + (struct(16, 8, 128),),
        fields + (from_east, from_west, from_south, from_north, parts),
    )
    parts = loading_parts(mass)
    return call(
        last_kernel,
        "last",
        (struct(ROWS, COLS),) * 3 + (struct(NB, NB),),
        tuple(state) + (parts,),
    )


def solution(mesh):
    fine = Mesh(np.asarray(mesh.devices).reshape(4, 4, 4, 4, 2), ("zh", "y", "zl", "x", "c"))
    lat, lon = ("zh", "y"), ("zl", "x", "c")
    return jax.shard_map(
        body,
        mesh=fine,
        in_specs=(P(lat, lon),) * 5 + (P(lat, None, lon),),
        out_specs=(P(lat, lon),) * 4,
        check_vma=False,
    )
```

time: 2480 us -> 167 us (0.07)
  waiting for transfers between devices: 2150 us -> 23.4 us
  local copies, waits for them, and re-layouts: 139 us -> 2.3 us
  blocking collectives: 0 us -> 82.4 us
  other arithmetic: 76.9 us -> 0.08 us
  matrix products: 53 us -> 0 us
    all_gather x2 -> x0, waiting for transfers between devices: 1640 us -> none  [body(): everyone = lax.all_gather(mass[None], ('lat', 'lon'), axis=0, tiled=True)]
    unnamed x6 -> x0, waiting for transfers between devices: 509 us -> none
    all_to_all x0 -> x5, blocking collectives: none -> 82.4 us  [the longest x1 27.6 us: loading_parts(): column = lax.all_to_all(mass, ('zh', 'zl'), 0, 0, tiled=True)]
    while x736 -> x0, other arithmetic: 61.8 us -> none
    slice x760 -> x1, local copies, waits for them, and re-layouts: 56.7 us -> 0.01 us  [lat_message(): k = k2[:, edge_row].reshape(48, 256)]
    dot_general x32 -> x0, matrix products: 53 us -> none  [contract(): jnp.einsum('aje,ejx->ax', weights, stacked, precision=lax.Precision.HIGHEST)]
    dynamic_slice x32 -> x0, local copies, waits for them, and re-layouts: 28.7 us -> none  [band_term(): lax.dynamic_slice_in_dim(whole, first, CROWS, 0)]
  transfers between devices with their start and end apart: 12 -> 6, of which waited for: 5 -> 3; matrix products, arithmetic and copies ran while one was open for 0% -> 0% of each run, Pallas kernels for 0% -> 0%
where the time goes in v1:
time: 167 us; the launch traced here: 166 us
  blocking collectives  82.4 us (49%)
  starting transfers between devices  37.1 us (22%)
  waiting for transfers between devices  23.4 us (14%)
  Pallas kernels  19.6 us (12%)
  local copies, waits for them, and re-layouts  2.3 us (1%)
    all_to_all x1, blocking collectives, loading_parts(): column = lax.all_to_all(mass, ('zh', 'zl'), 0, 0, tiled=True)  27.6 us
    all_to_all x2, blocking collectives, loading_parts(): return lax.all_to_all(partial, LON, 0, 0, tiled=True)  26.8 us
    all_to_all x1, blocking collectives, loading_parts(): tiles = lax.all_to_all(spreadout, ('y', 'x', 'c'), 0, 0, tiled=True)  22.7 us
    pallas_call x5, Pallas kernels, call(): pl.pallas_call(kernel, name=name, out_shape=outs, in_specs=[VM] * len(ins...  19.6 us
    all_to_all x1, starting transfers between devices, loading_parts(): column = lax.all_to_all(mass, ('zh', 'zl'), 0, 0, tiled=True)  12.2 us
    all_to_all x1, waiting for transfers between devices, loading_parts(): column = lax.all_to_all(mass, ('zh', 'zl'), 0, 0, tiled=True)  11.6 us
    ppermute x1, waiting for transfers between devices, body(): lax.ppermute(lat_message(to_south, 0, 0), LAT, [(i + 1, i) for i in range...  10.6 us
    all_to_all x1, starting transfers between devices, loading_parts(): tiles = lax.all_to_all(spreadout, ('y', 'x', 'c'), 0, 0, tiled=True)  8.9 us
  transfers between devices with their start and end apart: 6, of which 3 were waited for; matrix products, arithmetic and copies ran while one was open for 0% of the time, Pallas kernels for 0%

profile of v1, /device:TPU:1, one launch (start us, length us, event | category | flops | bytes accessed | tf_op | source)
XLA Modules:
  0.0 165.7 jit_solution(7296381258326116866)
XLA Ops:
  0.6 0.0 copy-start.2
  0.6 2.6 %pack.1 = (f32[16,8,128]{2,1,0:T(8,128)}, f32[192,128]{1,0:T(8,128)}, f32[192,128]{1,0:T(8,128)}, f32[120,128]{1,0:T(8,128)}, f32[120,128]{1,0:T(8,128)}) custom-call(f32[192,384]{1,0:T(8,128)} %h_ref.3, f32[192,384]{1,0:T(8,128)} %fl_ref.3, f32[192,384]{1,0:T(8,128)} %ft_ref.3, f32[192,384]{1,0:T(8,128)} %d_ref.3, s32[192,384]{1,0:T(8,128)} %wet_ref.3), custom_call_target="tpu_custom_call" | custom-call | tf_op jit(solution)/shard_map/pack/pallas_call | solution.py:262
  3.3 8.8 %collective-permute-start = (f32[192,128]{1,0:T(8,128)}, f32[192,128]{1,0:T(8,128)S(1)}, u32[]{:S(2)}, u32[]{:S(2)}) collective-permute-start(f32[192,128]{1,0:T(8,128)} %get-tuple-element.15), channel_id=1, source_target_pairs={{1,0},{2,1},{3,2},{4,3},{5,4},{6,5},{7,6},{8,7},{9,8},{10,9},{11,1... | collective-permute-start | bytes 294920 | tf_op jit(solution)/shard_map/ppermute | solution.py:286
  12.1 1.9 %collective-permute-start.1 = (f32[192,128]{1,0:T(8,128)}, f32[192,128]{1,0:T(8,128)S(1)}, u32[]{:S(2)}, u32[]{:S(2)}) collective-permute-start(f32[192,128]{1,0:T(8,128)} %get-tuple-element.16), channel_id=1, source_target_pairs={{0,1},{1,2},{2,3},{3,4},{4,5},{5,6},{6,7},{7,8},{8,9},{9,10},{10,1... | collective-permute-start | bytes 294920 | tf_op jit(solution)/shard_map/ppermute | solution.py:285
  14.0 0.0 copy-done.2
  14.0 0.1 slice_bitcast_fusion.1
  14.1 0.1 pad_maximum_fusion
  14.2 5.3 %all_to_all.35.k_ref = f32[2,24,24,256]{3,2,1,0:T(8,128)S(1)} all-to-all(f32[2,24,24,256]{3,2,1,0:T(8,128)S(1)} %pad_maximum_fusion), channel_id=1, replica_groups=mesh['zh'=4,'y'=4,'zl'=4,'x'=4,'c'=2] {'c'}, dimensions={0} | all-to-all | bytes 2359296 | tf_op jit(solution)/shard_map/all_to_all | solution.py:287
  19.5 12.2 %all-to-all-start.1 = ((f32[16,8,128]{2,1,0:T(8,128)}), f32[16,8,128]{2,1,0:T(8,128)S(1)}, u32[]{:S(2)}, u32[]{:S(2)}) async-start(f32[16,8,128]{2,1,0:T(8,128)} %get-tuple-element.19), calls=%async_computation.1 | async-start | bytes 131072 | tf_op jit(solution)/shard_map/all_to_all | solution.py:299
  31.8 0.0 collective-permute-done.fe_ref
  31.8 0.0 collective-permute-done.1.fw_ref
  31.8 0.0 copy-start.6
  31.9 11.6 %all-to-all-done.1 = f32[16,8,128]{2,1,0:T(8,128)S(1)} async-done(((f32[16,8,128]{2,1,0:T(8,128)}), f32[16,8,128]{2,1,0:T(8,128)S(1)}, u32[]{:S(2)}, u32[]{:S(2)}) %all-to-all-start.1) | async-done | bytes 65568 | tf_op jit(solution)/shard_map/all_to_all | solution.py:299
  43.4 1.1 broadcast_in_dim.15
  44.5 0.0 copy-done.6
  44.5 8.9 %all-to-all-start.2 = ((f32[32,64,128]{2,1,0:T(8,128)}), f32[32,64,128]{2,1,0:T(8,128)S(1)}, u32[]{:S(2)}, u32[]{:S(2)}) async-start(f32[32,64,128]{2,1,0:T(8,128)} %bitcast.6), calls=%async_computation.2 | async-start | bytes 2097152 | tf_op jit(solution)/shard_map/all_to_all | solution.py:301
  53.5 1.3 collective-permute-start.3
  54.8 4.0 %collective-permute-start.2 = (f32[232,128]{1,0:T(8,128)S(1)}, f32[232,128]{1,0:T(8,128)S(1)}, u32[]{:S(2)}, u32[]{:S(2)}) collective-permute-start(f32[232,128]{1,0:T(8,128)S(1)} %slice_dynamic-update-slice_fusion.2), channel_id=1, source_target_pairs={{0,32},{32,64},{64,96},{96,128},{128,160},{160,192},{192,224},{224... | collective-permute-start | bytes 356360 | tf_op jit(solution)/shard_map/ppermute | solution.py:295
  58.8 10.6 %collective-permute-done.3.kn_ref.fn_ref = f32[232,128]{1,0:T(8,128)S(1)} collective-permute-done((f32[232,128]{1,0:T(8,128)S(1)}, f32[232,128]{1,0:T(8,128)S(1)}, u32[]{:S(2)}, u32[]{:S(2)}) %collective-permute-start.3) | collective-permute-done | bytes 118816 | tf_op jit(solution)/shard_map/ppermute | solution.py:296
  69.3 0.0 collective-permute-done.2.ks_ref.fs_ref
  69.3 1.3 all-to-all-done.2
  70.6 0.0 copy-done.3
  70.6 1.0 copy-done.1
  71.6 5.1 %conv.2 = f32[32,8,128]{2,1,0:T(8,128)} custom-call(f32[32,8,8,128]{3,2,1,0:T(8,128)} %bitcast.13, f32[2,24,24,256]{3,2,1,0:T(8,128)} %copy-done, f32[232,128]{1,0:T(8,128)} %copy-done.4, f32[232,128]{1,0:T(8,128)} %copy-done.3), custom_call_target="tpu_custom_call" | custom-call | tf_op jit(solution)/shard_map/conv/pallas_call | solution.py:262
  76.7 13.6 %all_to_all.36.rs_ref = f32[32,8,128]{2,1,0:T(8,128)} all-to-all(f32[32,8,128]{2,1,0:T(8,128)} %conv.2), channel_id=1, replica_groups=mesh['zh'=4,'y'=4,'zl'=4,'x'=4,'c'=2] {'zl','x','c'}, dimensions={0} | all-to-all | bytes 262144 | tf_op jit(solution)/shard_map/all_to_all | solution.py:309
  90.3 3.7 %first.1 = (f32[200,512]{1,0:T(8,128)}, f32[200,512]{1,0:T(8,128)}, f32[200,512]{1,0:T(8,128)}, f32[200,512]{1,0:T(8,128)}, f32[200,512]{1,0:T(8,128)}, /*index=5*/f32[16,8,128]{2,1,0:T(8,128)}) custom-call(f32[192,384]{1,0:T(8,128)} %h_ref.3, f32[192,384]{1,0:T(8,128)} %fl_ref.3, f32[192,384]{1,0:T(8,128)} %ft_ref.3, f32[192,384]{1,0:T(8,128)} %d_ref.3, ...), custom_call_target="tpu_custom_call" | custom-call | tf_op jit(solution)/shard_map/first/pallas_call | solution.py:262
  94.0 27.6 %all_to_all.37 = f32[16,8,128]{2,1,0:T(8,128)S(1)} all-to-all(f32[16,8,128]{2,1,0:T(8,128)} %get-tuple-element.25), channel_id=1, replica_groups=mesh['zh'=4,'y'=4,'zl'=4,'x'=4,'c'=2] {'zh','zl'}, dimensions={0} | all-to-all | bytes 131072 | tf_op jit(solution)/shard_map/all_to_all | solution.py:299
  121.6 0.1 broadcast_in_dim.17
  121.7 22.7 %all_to_all.38 = f32[32,64,128]{2,1,0:T(8,128)} all-to-all(f32[32,64,128]{2,1,0:T(8,128)S(1)} %bitcast.15), channel_id=1, replica_groups=mesh['zh'=4,'y'=4,'zl'=4,'x'=4,'c'=2] {'y','x','c'}, dimensions={0} | all-to-all | bytes 2097152 | tf_op jit(solution)/shard_map/all_to_all | solution.py:301
  144.4 5.1 %conv.3 = f32[32,8,128]{2,1,0:T(8,128)} custom-call(f32[32,8,8,128]{3,2,1,0:T(8,128)} %bitcast.14, f32[2,24,24,256]{3,2,1,0:T(8,128)} %copy-done, f32[232,128]{1,0:T(8,128)} %copy-done.4, f32[232,128]{1,0:T(8,128)} %copy-done.3), custom_call_target="tpu_custom_call" | custom-call | tf_op jit(solution)/shard_map/conv/pallas_call | solution.py:262
  149.5 13.2 %all_to_all.39.rs_ref = f32[32,8,128]{2,1,0:T(8,128)} all-to-all(f32[32,8,128]{2,1,0:T(8,128)} %conv.3), channel_id=1, replica_groups=mesh['zh'=4,'y'=4,'zl'=4,'x'=4,'c'=2] {'zl','x','c'}, dimensions={0} | all-to-all | bytes 262144 | tf_op jit(solution)/shard_map/all_to_all | solution.py:309
  162.7 3.0 %last.1 = (f32[192,384]{1,0:T(8,128)}, f32[192,384]{1,0:T(8,128)}, f32[192,384]{1,0:T(8,128)}, f32[24,24]{1,0:T(8,128)}) custom-call(f32[200,512]{1,0:T(8,128)} %get-tuple-element.20.h_ref, f32[200,512]{1,0:T(8,128)} %get-tuple-element.21.fl_ref, f32[200,512]{1,0:T(8,128)} %get-tuple-element.22.ft_ref, f32[200,512]{1,0:T(8,128)} %get-tuple-element.23.d_ref, ...), custom_call_target="tpu_custom_call" | custom-call | tf_op jit(solution)/shard_map/last/pallas_call | solution.py:262
  (20 shorter events, 0.1 us)
Async XLA Ops:
  0.6 13.4 %copy-start.2 = (f32[24,384,24]{1,2,0:T(8,128)S(1)}, f32[24,384,24]{1,2,0:T(8,128)}, u32[]{:S(2)}) copy-start(f32[24,384,24]{1,2,0:T(8,128)} %param.11) | copy-start | bytes 2654212
  3.3 28.5 %collective-permute-start = (f32[192,128]{1,0:T(8,128)}, f32[192,128]{1,0:T(8,128)S(1)}, u32[]{:S(2)}, u32[]{:S(2)}) collective-permute-start(f32[192,128]{1,0:T(8,128)} %get-tuple-element.15), channel_id=1, source_target_pairs={{1,0},{2,1},{3,2},{4,3},{5,4},{6,5},{7,6},{8,7},{9,8},{10,9},{11,1... | collective-permute-start | bytes 294920 | tf_op jit(solution)/shard_map/ppermute | solution.py:286
  12.1 19.8 %collective-permute-start.1 = (f32[192,128]{1,0:T(8,128)}, f32[192,128]{1,0:T(8,128)S(1)}, u32[]{:S(2)}, u32[]{:S(2)}) collective-permute-start(f32[192,128]{1,0:T(8,128)} %get-tuple-element.16), channel_id=1, source_target_pairs={{0,1},{1,2},{2,3},{3,4},{4,5},{5,6},{6,7},{7,8},{8,9},{9,10},{10,1... | collective-permute-start | bytes 294920 | tf_op jit(solution)/shard_map/ppermute | solution.py:285
  14.2 17.6 %copy-start.7 = (f32[120,128]{1,0:T(8,128)S(1)}, f32[120,128]{1,0:T(8,128)}, u32[]{:S(2)}) copy-start(f32[120,128]{1,0:T(8,128)} %get-tuple-element.17) | copy-start | bytes 184324
  14.2 17.6 %copy-start.8 = (f32[120,128]{1,0:T(8,128)S(1)}, f32[120,128]{1,0:T(8,128)}, u32[]{:S(2)}) copy-start(f32[120,128]{1,0:T(8,128)} %get-tuple-element.18) | copy-start | bytes 184324
  19.5 25.0 %copy-start = (f32[2,24,24,256]{3,2,1,0:T(8,128)}, f32[2,24,24,256]{3,2,1,0:T(8,128)S(1)}, u32[]{:S(2)}) copy-start(f32[2,24,24,256]{3,2,1,0:T(8,128)S(1)} %all_to_all.35.k_ref) | copy-start | bytes 3538948
  19.5 23.9 %all-to-all-start.1 = ((f32[16,8,128]{2,1,0:T(8,128)}), f32[16,8,128]{2,1,0:T(8,128)S(1)}, u32[]{:S(2)}, u32[]{:S(2)}) async-start(f32[16,8,128]{2,1,0:T(8,128)} %get-tuple-element.19), calls=%async_computation.1 | async-start | bytes 131072 | tf_op jit(solution)/shard_map/all_to_all | solution.py:299
  31.8 12.7 %copy-start.5 = (f32[192,128]{1,0:T(8,128)}, f32[192,128]{1,0:T(8,128)S(1)}, u32[]{:S(2)}) copy-start(f32[192,128]{1,0:T(8,128)S(1)} %collective-permute-done.fe_ref) | copy-start | bytes 294916
  31.8 12.7 %copy-start.6 = (f32[192,128]{1,0:T(8,128)}, f32[192,128]{1,0:T(8,128)S(1)}, u32[]{:S(2)}) copy-start(f32[192,128]{1,0:T(8,128)S(1)} %collective-permute-done.1.fw_ref) | copy-start | bytes 294916
  44.5 26.1 %all-to-all-start.2 = ((f32[32,64,128]{2,1,0:T(8,128)}), f32[32,64,128]{2,1,0:T(8,128)S(1)}, u32[]{:S(2)}, u32[]{:S(2)}) async-start(f32[32,64,128]{2,1,0:T(8,128)} %bitcast.6), calls=%async_computation.2 | async-start | bytes 2097152 | tf_op jit(solution)/shard_map/all_to_all | solution.py:301
  53.5 15.9 %collective-permute-start.3 = (f32[232,128]{1,0:T(8,128)S(1)}, f32[232,128]{1,0:T(8,128)S(1)}, u32[]{:S(2)}, u32[]{:S(2)}) collective-permute-start(f32[232,128]{1,0:T(8,128)S(1)} %slice_dynamic-update-slice_fusion), channel_id=1, source_target_pairs={{32,0},{64,32},{96,64},{128,96},{160,128},{192,160},{224,192},{256... | collective-permute-start | bytes 356360 | tf_op jit(solution)/shard_map/ppermute | solution.py:296
  54.8 14.6 %collective-permute-start.2 = (f32[232,128]{1,0:T(8,128)S(1)}, f32[232,128]{1,0:T(8,128)S(1)}, u32[]{:S(2)}, u32[]{:S(2)}) collective-permute-start(f32[232,128]{1,0:T(8,128)S(1)} %slice_dynamic-update-slice_fusion.2), channel_id=1, source_target_pairs={{0,32},{32,64},{64,96},{96,128},{128,160},{160,192},{192,224},{224... | collective-permute-start | bytes 356360 | tf_op jit(solution)/shard_map/ppermute | solution.py:295
  69.3 1.3 copy-start.3
  69.3 1.3 copy-start.4
  70.6 1.0 copy-start.1

commit v2 on v1

--- a/solution.py
+++ b/solution.py
@@ -13,7 +13,7 @@
 EROWS, ECOLS = 200, 512
 GRID_ROWS = 3072
 NB = 24
-HALO_TILES = 17
+HALO_TILES = 8
 STEP_ANGLE = math.pi / (180.0 * 240.0)
 COURANT = 0.3
 F32 = jnp.float32
@@ -46,14 +46,16 @@
     return tile
 
 
-def pack_kernel(h_ref, fl_ref, ft_ref, d_ref, wet_ref, mass_ref, east_ref, west_ref, north_ref, south_ref):
-    w = wet_ref[...].astype(F32)
-    fields = (h_ref[...], fl_ref[...], ft_ref[...], d_ref[...], w)
+def mass_kernel(h_ref, wet_ref, mass_ref):
     row = (lat_index() * ROWS + iota((ROWS, 128), 0)).astype(F32)
     cosc = jnp.concatenate([cos_row(row + 0.5)] * 3, axis=1)
-    tile = mass_tile(fields[0] * w * cosc)
+    tile = mass_tile(h_ref[...] * wet_ref[...].astype(F32) * cosc)
     for z in range(16):
         mass_ref[z] = tile
+
+
+def pack_kernel(h_ref, fl_ref, ft_ref, d_ref, wet_ref, east_ref, west_ref, north_ref, south_ref):
+    fields = (h_ref[...], fl_ref[...], ft_ref[...], d_ref[...], wet_ref[...].astype(F32))
     lane = iota((ROWS, 128), 1)
     east = jnp.zeros((ROWS, 128), F32)
     west = jnp.zeros((ROWS, 128), F32)
@@ -64,66 +66,98 @@
             last = pltpu.roll(last, 128 - 2 * f, 1)
         west = jnp.where((lane >= 2 * f) & (lane < 2 * f + 2), first, west)
         east = jnp.where((lane >= 126 - 2 * f) & (lane < 128 - 2 * f), last, east)
-        for t in range(3):
-            at = 8 * (3 * f + t)
-            north_ref[at : at + 8, :] = x[ROWS - 8 :, 128 * t : 128 * t + 128]
-            south_ref[at : at + 8, :] = x[:8, 128 * t : 128 * t + 128]
     east_ref[...] = east
     west_ref[...] = west
-
-
-def conv_kernel(mt_ref, k_ref, ks_ref, kn_ref, out_ref, m_ref, s_ref):
+    sub = iota((8, 128), 0)
+    for t in range(3):
+        for out, at, first in ((north_ref, ROWS - 8, 6), (south_ref, 0, 0)):
+            group = None
+            for f in range(4):
+                x = fields[f][at : at + 8, 128 * t : 128 * t + 128]
+                shift = (2 * f - first) % 8
+                x = pltpu.roll(x, shift, 0) if shift else x
+                group = x if f == 0 else jnp.where(sub >= 2 * f, x, group)
+            out[8 * t : 8 * t + 8, :] = group
+            out[24 + 8 * t : 32 + 8 * t, :] = fields[4][at : at + 8, 128 * t : 128 * t + 128]
+
+
+def repack_kernel(in_ref, out_ref):
+    lane = iota((8, 128), 1)
+    for c in range(2):
+        parts = [None] * 5
+        for n in range(24):
+            j, q = divmod(n, 3)
+            t, g = divmod(n, 5)
+            shift = (24 * g - 24 * q) % 128
+            piece = in_ref[8 * c + j]
+            piece = pltpu.roll(piece, shift, 1) if shift else piece
+            parts[t] = jnp.where(lane >= 24 * g, piece, parts[t]) if g else piece
+        for d in range(16):
+            for t in range(5):
+                out_ref[2 * d + c, :, 128 * t : 128 * t + 128] = parts[t]
+
+
+def split(x):
+    high = x.astype(BF16)
+    return high, (x - high.astype(F32)).astype(BF16)
+
+
+def product(wide, mh, ml):
+    wh, wl = split(wide)
+    return (
+        jnp.dot(wh, mh, preferred_element_type=F32)
+        + jnp.dot(wh, ml, preferred_element_type=F32)
+        + jnp.dot(wl, mh, preferred_element_type=F32)
+    )
+
+
+def lagged(first, second):
+    total = pltpu.roll(first, 0, 1, stride=1, stride_axis=0) + pltpu.roll(
+        second, 24, 1, stride=1, stride_axis=0
+    )
+    return jnp.sum(total, axis=0, keepdims=True)
+
+
+def conv_rows(mt_ref, k_ref, m_ref, s_ref):
     core = lax.axis_index("c")
     lane = iota((8, 128), 1)
     m_ref[...] = jnp.zeros_like(m_ref)
-    for yl in range(8):
-        zh, y = yl // 4, yl % 4
+    for j in range(8):
+        zh, y = divmod(j, 4)
         for q in range(3):
             parts = [None] * 6
             for b in range(32):
-                zl, xc = b // 8, b % 8
-                src = mt_ref[y * 8 + xc, zh * 4 + zl]
+                zl, xc = divmod(b, 8)
+                i, g = divmod(3 * (4 * zh + zl) + q, 5)
                 t, o = divmod(24 * b, 128)
-                shift = (24 * b - 24 * q) % 128
+                shift = (24 * b - 24 * g) % 128
+                src = mt_ref[8 * y + xc, :, 128 * i : 128 * i + 128]
                 src = pltpu.roll(src, shift, 1) if shift else src
                 parts[t] = jnp.where(lane >= o, src, parts[t]) if o else src
                 if o + 24 > 128:
                     parts[t + 1] = src
-            rows = jnp.concatenate(parts, axis=1)
-            m_ref[pl.ds(pl.multiple_of(core * 64 + (yl * 24 + q * 8), 8), 8), :] = rows
-    m = m_ref[...]
-    mh = m.astype(BF16)
-    ml = (m - mh.astype(F32)).astype(BF16)
-
-    def product(wide):
-        wh = wide.astype(BF16)
-        wl = (wide - wh.astype(F32)).astype(BF16)
-        return (
-            jnp.dot(wh, mh, preferred_element_type=F32)
-            + jnp.dot(wh, ml, preferred_element_type=F32)
-            + jnp.dot(wl, mh, preferred_element_type=F32)
-        )
-
-    def lagged(first, second):
-        total = pltpu.roll(first, 0, 1, stride=1, stride_axis=0) + pltpu.roll(
-            second, 24, 1, stride=1, stride_axis=0
-        )
-        return jnp.sum(total, axis=0, keepdims=True)
-
+            at = pl.multiple_of(core * 64 + (24 * j + 8 * q), 8)
+            m_ref[pl.ds(at, 8), :] = jnp.concatenate(parts, axis=1)
+    mh, ml = split(m_ref[...])
     per = 4
     for group in range(NB // per):
         wide = jnp.concatenate(
             [k_ref[s, per * group : per * group + per].reshape(per * NB, 256) for s in range(2)], axis=0
         )
-        p = product(wide)
+        p = product(wide, mh, ml)
         for i in range(per):
             a = per * group + i
             s_ref[a + 1 : a + 2, :] = lagged(p[NB * i : NB * i + NB], p[NB * (per + i) : NB * (per + i) + NB])
+    return mh, ml
+
+
+def conv_edges(mh, ml, ks_ref, kn_ref, s_ref, out_ref):
+    lane = iota((8, 128), 1)
     wide = jnp.concatenate(
         [jnp.concatenate([r[8 * HALO_TILES : 8 * HALO_TILES + 48], r[8 * HALO_TILES + 48 :]], axis=1) for r in (ks_ref, kn_ref)],
         axis=0,
     )
-    p = product(wide)
+    p = product(wide, mh, ml)
     s_ref[0:1, :] = lagged(p[0:24], p[24:48])
     s_ref[25:26, :] = lagged(p[48:72], p[72:96])
     s_ref[26:32, :] = jnp.zeros((6, 768), F32)
@@ -144,6 +178,21 @@
         out_ref[lax.rem(base + k, 32)] = jnp.where(lane < 104, message, 0.0)
 
 
+def conv_kernel(mt_ref, k_ref, ks_ref, kn_ref, out_ref, m_ref, s_ref):
+    mh, ml = conv_rows(mt_ref, k_ref, m_ref, s_ref)
+    conv_edges(mh, ml, ks_ref, kn_ref, s_ref, out_ref)
+
+
+def own_kernel(mt_ref, k_ref, rows_ref, mh_ref, ml_ref, m_ref, s_ref):
+    mh_ref[...], ml_ref[...] = conv_rows(mt_ref, k_ref, m_ref, s_ref)
+    rows_ref[...] = s_ref[1:25, :]
+
+
+def edge_kernel(rows_ref, mh_ref, ml_ref, ks_ref, kn_ref, out_ref, s_ref):
+    s_ref[1:25, :] = rows_ref[...]
+    conv_edges(mh_ref[...], ml_ref[...], ks_ref, kn_ref, s_ref, out_ref)
+
+
 def loading_tile(rs_ref):
     parts = [rs_ref[i] for i in range(32)]
     while len(parts) > 1:
@@ -220,14 +269,17 @@
             w = pltpu.roll(w, 2 * f, 1)
         return jnp.where(at < 2, e, jnp.where(at >= 126, w, 0.0))
 
-    def edge(ref, f):
-        tiles = [ref[8 * (3 * f + t) : 8 * (3 * f + t) + 8, :] for t in range(3)]
-        return tiles + [side(ref[120:128, :], ref[128:136, :], f, lane8)]
+    def edge(ref, f, first):
+        at = 0 if f < 4 else 24
+        tiles = [ref[at + 8 * t : at + 8 * t + 8, :] for t in range(3)]
+        shift = (first - 2 * f) % 8 if f < 4 else 0
+        tiles = [pltpu.roll(x, shift, 0) for x in tiles] if shift else tiles
+        return tiles + [side(ref[48:56, :], ref[56:64, :], f, lane8)]
 
     ext = []
     for f, x in enumerate((h_ref[...], fl_ref[...], ft_ref[...], d_ref[...], wet_ref[...].astype(F32))):
         main = jnp.concatenate([x, side(fe_ref[...], fw_ref[...], f, lane)], axis=1)
-        from_south, from_north = edge(fs_ref, f), edge(fn_ref, f)
+        from_south, from_north = edge(fs_ref, f, 6), edge(fn_ref, f, 0)
         tail = jnp.concatenate(
             [jnp.where(sub8 < 4, n, s) for n, s in zip(from_north, from_south)], axis=1
         )
@@ -272,20 +324,24 @@
 def body(height, flux_lon, flux_lat, depth, wet, kernel):
     LAT, LON = ("zh", "y"), ("zl", "x", "c")
     fields = (height, flux_lon, flux_lat, depth, wet)
-    halves = kernel.transpose(0, 2, 1)
-    halves = jnp.stack([halves[:, :, :256], halves[:, :, 128:]])
-    mass, to_east, to_west, to_north, to_south = call(
+    mass = call(mass_kernel, "mass", struct(16, 8, 128), (height, wet))
+    mass, *tied = lax.optimization_barrier((mass, kernel, *fields))
+    to_east, to_west, to_north, to_south = call(
         pack_kernel,
         "pack",
-        (struct(16, 8, 128), struct(ROWS, 128), struct(ROWS, 128), struct(120, 128), struct(120, 128)),
-        fields,
-    )
-    up = [(i, (i + 1) % 32) for i in range(32)]
-    down = [((i + 1) % 32, i) for i in range(32)]
-    from_west = lax.ppermute(to_east, LON, up)
-    from_east = lax.ppermute(to_west, LON, down)
+        (struct(ROWS, 128), struct(ROWS, 128), struct(48, 128), struct(48, 128)),
+        tied[1:],
+    )
+    from_west = lax.ppermute(to_east, LON, [(i, (i + 1) % 32) for i in range(32)])
+    from_east = lax.ppermute(to_west, LON, [((i + 1) % 32, i) for i in range(32)])
+    column = lax.all_to_all(mass, ("zh", "zl"), 0, 0, tiled=True)
+    turned = tied[0].transpose(0, 2, 1)
+    halves = jnp.stack([turned[:, :, :256], turned[:, :, 128:]])
+    column, from_west, from_east, halves = lax.optimization_barrier((column, from_west, from_east, halves))
     k2 = lax.all_to_all(halves, "c", 0, 0, tiled=True)
 
+    column = call(repack_kernel, "repack", struct(32, 8, 640), (column,))
+    column, k2 = lax.optimization_barrier((column, k2))
     def lat_message(rows, at, edge_row):
         k = k2[:, edge_row].reshape(48, 256)
         return jnp.concatenate(
@@ -295,27 +351,23 @@
     from_south = lax.ppermute(lat_message(to_north, ROWS - 8, 23), LAT, [(i, i + 1) for i in range(15)])
     from_north = lax.ppermute(lat_message(to_south, 0, 0), LAT, [(i + 1, i) for i in range(15)])
 
-    def loading_parts(mass):
-        column = lax.all_to_all(mass, ("zh", "zl"), 0, 0, tiled=True)
-        spreadout = jnp.broadcast_to(column.reshape(1, 2, 64, 128), (16, 2, 64, 128)).reshape(32, 64, 128)
-        tiles = lax.all_to_all(spreadout, ("y", "x", "c"), 0, 0, tiled=True)
-        partial = call(
-            conv_kernel,
-            "conv",
-            struct(32, 8, 128),
-            (tiles.reshape(32, 8, 8, 128), k2, from_south, from_north),
-            (pltpu.VMEM((256, 768), F32), pltpu.VMEM((32, 768), F32)),
-        )
-        return lax.all_to_all(partial, LON, 0, 0, tiled=True)
-
-    parts = loading_parts(mass)
+    tiles = lax.all_to_all(column, ("y", "x", "c"), 0, 0, tiled=True)
+    wide, coarse = pltpu.VMEM((256, 768), F32), pltpu.VMEM((32, 768), F32)
+    half = jax.ShapeDtypeStruct((256, 768), BF16)
+    own = call(own_kernel, "own", (struct(NB, 768), half, half), (tiles, k2), (wide, coarse))
+    parts = call(edge_kernel, "edge", struct(32, 8, 128), (*own, from_south, from_north), (coarse,))
+    parts = lax.all_to_all(parts, LON, 0, 0, tiled=True)
     *state, mass = call(
         first_kernel,
         "first",
         (struct(EROWS, ECOLS),) * 5 + (struct(16, 8, 128),),
         fields + (from_east, from_west, from_south, from_north, parts),
     )
-    parts = loading_parts(mass)
+    column = lax.all_to_all(mass, ("zh", "zl"), 0, 0, tiled=True)
+    column = call(repack_kernel, "repack", struct(32, 8, 640), (column,))
+    tiles = lax.all_to_all(column, ("y", "x", "c"), 0, 0, tiled=True)
+    parts = call(conv_kernel, "conv", struct(32, 8, 128), (tiles, k2, from_south, from_north), (wide, coarse))
+    parts = lax.all_to_all(parts, LON, 0, 0, tiled=True)
     return call(
         last_kernel,
         "last",

time: 167 us -> 158 us (0.946)
  waiting for transfers between devices: 23.4 us -> 10.8 us
  Pallas kernels: 19.6 us -> 27 us
  blocking collectives: 82.4 us -> 75.8 us
  starting transfers between devices: 37.1 us -> 39.8 us
    ppermute x1, waiting for transfers between devices: 10.6 us -> 0.01 us  [body(): lax.ppermute(lat_message(to_south, 0, 0), LAT, [(i + 1, i) for i in range...]
    all_to_all x2 -> x3, starting transfers between devices: 21.1 us -> 28.7 us  [the longest x1 15.7 us: body(): column = lax.all_to_all(mass, ('zh', 'zl'), 0, 0, tiled=True)]
    pallas_call x5 -> x9, Pallas kernels: 19.6 us -> 27 us  [call(): pl.pallas_call(kernel, name=name, out_shape=outs, in_specs=[VM] * len(ins...]
    all_to_all x5 -> x4, blocking collectives: 82.4 us -> 75.8 us  [the longest x2 28.5 us: body(): parts = lax.all_to_all(parts, LON, 0, 0, tiled=True)]
    all_to_all x2 -> x3, waiting for transfers between devices: 12.8 us -> 7.54 us  [the longest x1 7.5 us: body(): tiles = lax.all_to_all(column, ('y', 'x', 'c'), 0, 0, tiled=True)]
    ppermute x2, starting transfers between devices: 10.7 us -> 5.87 us  [the longest x1 3.95 us: body(): lax.ppermute(to_east, LON, [(i, (i + 1) % 32) for i in range(32)])]
    ppermute x2, waiting for transfers between devices: 0.01 us -> 3.23 us  [the longest x1 3.22 us: body(): lax.ppermute(to_west, LON, [((i + 1) % 32, i) for i in range(32)])]
  transfers between devices with their start and end apart: 6 -> 7, of which waited for: 3 -> 2; matrix products, arithmetic and copies ran while one was open for 0% -> 1% of each run, Pallas kernels for 0% -> 6%
where the time goes in v2:
time: 158 us; the launch traced here: 157 us
  blocking collectives  75.8 us (48%)
  starting transfers between devices  39.8 us (25%)
  Pallas kernels  27 us (17%)
  waiting for transfers between devices  10.8 us (7%)
  local copies, waits for them, and re-layouts  1.64 us (1%)
    all_to_all x2, blocking collectives, body(): parts = lax.all_to_all(parts, LON, 0, 0, tiled=True)  28.5 us
    all_to_all x1, blocking collectives, body(): column = lax.all_to_all(mass, ('zh', 'zl'), 0, 0, tiled=True)  28 us
    pallas_call x9, Pallas kernels, call(): pl.pallas_call(kernel, name=name, out_shape=outs, in_specs=[VM] * len(ins...  27 us
    all_to_all x1, blocking collectives, body(): tiles = lax.all_to_all(column, ('y', 'x', 'c'), 0, 0, tiled=True)  19.3 us
    all_to_all x1, starting transfers between devices, body(): column = lax.all_to_all(mass, ('zh', 'zl'), 0, 0, tiled=True)  15.7 us
    all_to_all x1, waiting for transfers between devices, body(): tiles = lax.all_to_all(column, ('y', 'x', 'c'), 0, 0, tiled=True)  7.5 us
    all_to_all x1, starting transfers between devices, body(): tiles = lax.all_to_all(column, ('y', 'x', 'c'), 0, 0, tiled=True)  6.82 us
    all_to_all x1, starting transfers between devices, body(): k2 = lax.all_to_all(halves, 'c', 0, 0, tiled=True)  6.13 us
  transfers between devices with their start and end apart: 7, of which 2 were waited for; matrix products, arithmetic and copies ran while one was open for 1% of the time, Pallas kernels for 6%

profile of v2, /device:TPU:1, one launch (start us, length us, event | category | flops | bytes accessed | tf_op | source)
XLA Modules:
  0.0 157.0 jit_solution(14493668875709425938)
XLA Ops:
  0.6 2.3 %mass.1 = f32[16,8,128]{2,1,0:T(8,128)} custom-call(f32[192,384]{1,0:T(8,128)} %h_ref.4, s32[192,384]{1,0:T(8,128)} %wet_ref.4), custom_call_target="tpu_custom_call" | custom-call | tf_op jit(solution)/shard_map/mass/pallas_call | solution.py:314
  2.9 15.7 %all-to-all-start = ((f32[16,8,128]{2,1,0:T(8,128)}), f32[16,8,128]{2,1,0:T(8,128)S(1)}, u32[]{:S(2)}, u32[]{:S(2)}) async-start(f32[16,8,128]{2,1,0:T(8,128)} %mass.1), calls=%async_computation | async-start | bytes 131072 | tf_op jit(solution)/shard_map/all_to_all | solution.py:337
  18.7 2.3 %pack.1 = (f32[192,128]{1,0:T(8,128)}, f32[192,128]{1,0:T(8,128)}, f32[48,128]{1,0:T(8,128)}, f32[48,128]{1,0:T(8,128)}) custom-call(f32[192,384]{1,0:T(8,128)} %h_ref.4, f32[192,384]{1,0:T(8,128)} %fl_ref.2, f32[192,384]{1,0:T(8,128)} %ft_ref.2, f32[192,384]{1,0:T(8,128)} %d_ref.2, s32[192,384]{1,0:T(8,128)} %wet_ref.4), custom_call_target="tpu_custom_call" | custom-call | tf_op jit(solution)/shard_map/pack/pallas_call | solution.py:314
  20.9 4.0 %collective-permute-start = (f32[192,128]{1,0:T(8,128)}, f32[192,128]{1,0:T(8,128)S(1)}, u32[]{:S(2)}, u32[]{:S(2)}) collective-permute-start(f32[192,128]{1,0:T(8,128)} %get-tuple-element.36), channel_id=1, source_target_pairs={{0,1},{1,2},{2,3},{3,4},{4,5},{5,6},{6,7},{7,8},{8,9},{9,10},{10,1... | collective-permute-start | bytes 294920 | tf_op jit(solution)/shard_map/ppermute | solution.py:335
  24.9 1.9 %collective-permute-start.1 = (f32[192,128]{1,0:T(8,128)}, f32[192,128]{1,0:T(8,128)S(1)}, u32[]{:S(2)}, u32[]{:S(2)}) collective-permute-start(f32[192,128]{1,0:T(8,128)} %get-tuple-element.37), channel_id=1, source_target_pairs={{1,0},{2,1},{3,2},{4,3},{5,4},{6,5},{7,6},{8,7},{9,8},{10,9},{11,1... | collective-permute-start | bytes 294920 | tf_op jit(solution)/shard_map/ppermute | solution.py:336
  26.8 0.1 slice_bitcast_fusion.1
  26.9 0.0 copy-start.8
  26.9 1.1 pad_maximum_fusion
  28.1 0.0 collective-permute-done.fw_ref
  28.1 0.0 copy-start.6
  28.1 3.2 %collective-permute-done.1.fe_ref = f32[192,128]{1,0:T(8,128)S(1)} collective-permute-done((f32[192,128]{1,0:T(8,128)}, f32[192,128]{1,0:T(8,128)S(1)}, u32[]{:S(2)}, u32[]{:S(2)}) %collective-permute-start.1) | collective-permute-done | bytes 98336 | tf_op jit(solution)/shard_map/ppermute | solution.py:336
  31.3 0.0 all-to-all-done.in_ref
  31.3 6.1 %all-to-all-start.1 = ((f32[2,24,24,256]{3,2,1,0:T(8,128)}), f32[2,24,24,256]{3,2,1,0:T(8,128)S(1)}, u32[]{:S(2)}, u32[]{:S(2)}) async-start(f32[2,24,24,256]{3,2,1,0:T(8,128)} %pad_maximum_fusion), calls=%async_computation.1 | async-start | bytes 2359296 | tf_op jit(solution)/shard_map/all_to_all | solution.py:341
  37.5 1.8 %repack.2 = f32[32,8,640]{2,1,0:T(8,128)} custom-call(f32[16,8,128]{2,1,0:T(8,128)} %copy-done.5), custom_call_target="tpu_custom_call" | custom-call | tf_op jit(solution)/shard_map/repack/pallas_call | solution.py:314
  39.3 0.0 all-to-all-done.1.k_ref
  39.3 6.8 %all-to-all-start.2 = ((f32[32,8,640]{2,1,0:T(8,128)}), f32[32,8,640]{2,1,0:T(8,128)S(1)}, u32[]{:S(2)}, u32[]{:S(2)}) async-start(f32[32,8,640]{2,1,0:T(8,128)} %repack.2), calls=%async_computation.2 | async-start | bytes 1310720 | tf_op jit(solution)/shard_map/all_to_all | solution.py:354
  46.3 1.3 collective-permute-start.3
  47.6 4.0 %collective-permute-start.2 = (f32[160,128]{1,0:T(8,128)S(1)}, f32[160,128]{1,0:T(8,128)S(1)}, u32[]{:S(2)}, u32[]{:S(2)}) collective-permute-start(f32[160,128]{1,0:T(8,128)S(1)} %slice_dynamic-update-slice_fusion.2), channel_id=1, source_target_pairs={{0,32},{32,64},{64,96},{96,128},{128,160},{160,192},{192,224},{224... | collective-permute-start | bytes 245768 | tf_op jit(solution)/shard_map/ppermute | solution.py:351
  51.6 7.5 %all-to-all-done.2.mt_ref = f32[32,8,640]{2,1,0:T(8,128)S(1)} async-done(((f32[32,8,640]{2,1,0:T(8,128)}), f32[32,8,640]{2,1,0:T(8,128)S(1)}, u32[]{:S(2)}, u32[]{:S(2)}) %all-to-all-start.2) | async-done | bytes 655392 | tf_op jit(solution)/shard_map/all_to_all | solution.py:354
  59.1 0.8 copy-done.1
  59.9 4.7 %own.1 = (f32[24,768]{1,0:T(8,128)}, bf16[256,768]{1,0:T(8,128)(2,1)}, bf16[256,768]{1,0:T(8,128)(2,1)}) custom-call(f32[32,8,640]{2,1,0:T(8,128)} %copy-done.1, f32[2,24,24,256]{3,2,1,0:T(8,128)} %copy-done), custom_call_target="tpu_custom_call" | custom-call | tf_op jit(solution)/shard_map/own/pallas_call | solution.py:314
  64.6 0.6 copy-done.3
  65.2 0.0 copy-done.4
  65.3 2.5 %edge.1 = f32[32,8,128]{2,1,0:T(8,128)} custom-call(f32[24,768]{1,0:T(8,128)} %get-tuple-element.47.rows_ref, bf16[256,768]{1,0:T(8,128)(2,1)} %get-tuple-element.48.mh_ref, bf16[256,768]{1,0:T(8,128)(2,1)} %get-tuple-element.49.ml_ref, f32[160,128]{1,0:T(8,128)} %copy-done.4, f32[160,128]{1,0:T(8,128)} %copy-done.3), custom_call_target="tpu_custom_call" | custom-call | tf_op jit(solution)/shard_map/edge/pallas_call | solution.py:314
  67.7 15.1 %all_to_all.35.rs_ref = f32[32,8,128]{2,1,0:T(8,128)} all-to-all(f32[32,8,128]{2,1,0:T(8,128)} %edge.1), channel_id=1, replica_groups=mesh['zh'=4,'y'=4,'zl'=4,'x'=4,'c'=2] {'zl','x','c'}, dimensions={0} | all-to-all | bytes 262144 | tf_op jit(solution)/shard_map/all_to_all | solution.py:359
  82.8 3.7 %first.1 = (f32[200,512]{1,0:T(8,128)}, f32[200,512]{1,0:T(8,128)}, f32[200,512]{1,0:T(8,128)}, f32[200,512]{1,0:T(8,128)}, f32[200,512]{1,0:T(8,128)}, /*index=5*/f32[16,8,128]{2,1,0:T(8,128)}) custom-call(f32[192,384]{1,0:T(8,128)} %h_ref.4, f32[192,384]{1,0:T(8,128)} %fl_ref.2, f32[192,384]{1,0:T(8,128)} %ft_ref.2, f32[192,384]{1,0:T(8,128)} %d_ref.2, ...), custom_call_target="tpu_custom_call" | custom-call | tf_op jit(solution)/shard_map/first/pallas_call | solution.py:314
  86.5 28.0 %all_to_all.36.in_ref = f32[16,8,128]{2,1,0:T(8,128)} all-to-all(f32[16,8,128]{2,1,0:T(8,128)} %get-tuple-element.55), channel_id=1, replica_groups=mesh['zh'=4,'y'=4,'zl'=4,'x'=4,'c'=2] {'zh','zl'}, dimensions={0} | all-to-all | bytes 131072 | tf_op jit(solution)/shard_map/all_to_all | solution.py:366
  114.6 1.8 %repack.3 = f32[32,8,640]{2,1,0:T(8,128)} custom-call(f32[16,8,128]{2,1,0:T(8,128)} %all_to_all.36.in_ref), custom_call_target="tpu_custom_call" | custom-call | tf_op jit(solution)/shard_map/repack/pallas_call | solution.py:314
  116.4 19.3 %all_to_all.37.mt_ref = f32[32,8,640]{2,1,0:T(8,128)} all-to-all(f32[32,8,640]{2,1,0:T(8,128)} %repack.3), channel_id=1, replica_groups=mesh['zh'=4,'y'=4,'zl'=4,'x'=4,'c'=2] {'y','x','c'}, dimensions={0} | all-to-all | bytes 1310720 | tf_op jit(solution)/shard_map/all_to_all | solution.py:368
  135.6 5.0 %conv.1 = f32[32,8,128]{2,1,0:T(8,128)} custom-call(f32[32,8,640]{2,1,0:T(8,128)} %all_to_all.37.mt_ref, f32[2,24,24,256]{3,2,1,0:T(8,128)} %copy-done, f32[160,128]{1,0:T(8,128)} %copy-done.4, f32[160,128]{1,0:T(8,128)} %copy-done.3), custom_call_target="tpu_custom_call" | custom-call | tf_op jit(solution)/shard_map/conv/pallas_call | solution.py:314
  140.6 13.4 %all_to_all.38.rs_ref = f32[32,8,128]{2,1,0:T(8,128)} all-to-all(f32[32,8,128]{2,1,0:T(8,128)} %conv.1), channel_id=1, replica_groups=mesh['zh'=4,'y'=4,'zl'=4,'x'=4,'c'=2] {'zl','x','c'}, dimensions={0} | all-to-all | bytes 262144 | tf_op jit(solution)/shard_map/all_to_all | solution.py:370
  154.0 3.0 %last.1 = (f32[192,384]{1,0:T(8,128)}, f32[192,384]{1,0:T(8,128)}, f32[192,384]{1,0:T(8,128)}, f32[24,24]{1,0:T(8,128)}) custom-call(f32[200,512]{1,0:T(8,128)} %get-tuple-element.50.h_ref, f32[200,512]{1,0:T(8,128)} %get-tuple-element.51.fl_ref, f32[200,512]{1,0:T(8,128)} %get-tuple-element.52.ft_ref, f32[200,512]{1,0:T(8,128)} %get-tuple-element.53.d_ref, ...), custom_call_target="tpu_custom_call" | custom-call | tf_op jit(solution)/shard_map/last/pallas_call | solution.py:314
  (25 shorter events, 0.1 us)
Async XLA Ops:
  0.6 26.2 %copy-start.2 = (f32[24,384,24]{1,2,0:T(8,128)S(1)}, f32[24,384,24]{1,2,0:T(8,128)}, u32[]{:S(2)}) copy-start(f32[24,384,24]{1,2,0:T(8,128)} %param.11) | copy-start | bytes 2654212
  2.9 28.4 %all-to-all-start = ((f32[16,8,128]{2,1,0:T(8,128)}), f32[16,8,128]{2,1,0:T(8,128)S(1)}, u32[]{:S(2)}, u32[]{:S(2)}) async-start(f32[16,8,128]{2,1,0:T(8,128)} %mass.1), calls=%async_computation | async-start | bytes 131072 | tf_op jit(solution)/shard_map/all_to_all | solution.py:337
  20.9 7.2 %collective-permute-start = (f32[192,128]{1,0:T(8,128)}, f32[192,128]{1,0:T(8,128)S(1)}, u32[]{:S(2)}, u32[]{:S(2)}) collective-permute-start(f32[192,128]{1,0:T(8,128)} %get-tuple-element.36), channel_id=1, source_target_pairs={{0,1},{1,2},{2,3},{3,4},{4,5},{5,6},{6,7},{7,8},{8,9},{9,10},{10,1... | collective-permute-start | bytes 294920 | tf_op jit(solution)/shard_map/ppermute | solution.py:335
  24.9 6.4 %collective-permute-start.1 = (f32[192,128]{1,0:T(8,128)}, f32[192,128]{1,0:T(8,128)S(1)}, u32[]{:S(2)}, u32[]{:S(2)}) collective-permute-start(f32[192,128]{1,0:T(8,128)} %get-tuple-element.37), channel_id=1, source_target_pairs={{1,0},{2,1},{3,2},{4,3},{5,4},{6,5},{7,6},{8,7},{9,8},{10,9},{11,1... | collective-permute-start | bytes 294920 | tf_op jit(solution)/shard_map/ppermute | solution.py:336
  26.9 1.2 copy-start.8
  26.9 1.1 copy-start.9
  28.1 18.1 %copy-start.6 = (f32[192,128]{1,0:T(8,128)}, f32[192,128]{1,0:T(8,128)S(1)}, u32[]{:S(2)}) copy-start(f32[192,128]{1,0:T(8,128)S(1)} %collective-permute-done.fw_ref) | copy-start | bytes 294916
  31.3 14.8 %copy-start.7 = (f32[192,128]{1,0:T(8,128)}, f32[192,128]{1,0:T(8,128)S(1)}, u32[]{:S(2)}) copy-start(f32[192,128]{1,0:T(8,128)S(1)} %collective-permute-done.1.fe_ref) | copy-start | bytes 294916
  31.3 6.1 %copy-start.5 = (f32[16,8,128]{2,1,0:T(8,128)}, f32[16,8,128]{2,1,0:T(8,128)S(1)}, u32[]{:S(2)}) copy-start(f32[16,8,128]{2,1,0:T(8,128)S(1)} %all-to-all-done.in_ref) | copy-start | bytes 196612
  31.3 8.0 %all-to-all-start.1 = ((f32[2,24,24,256]{3,2,1,0:T(8,128)}), f32[2,24,24,256]{3,2,1,0:T(8,128)S(1)}, u32[]{:S(2)}, u32[]{:S(2)}) async-start(f32[2,24,24,256]{3,2,1,0:T(8,128)} %pad_maximum_fusion), calls=%async_computation.1 | async-start | bytes 2359296 | tf_op jit(solution)/shard_map/all_to_all | solution.py:341
  39.3 19.7 %copy-start = (f32[2,24,24,256]{3,2,1,0:T(8,128)}, f32[2,24,24,256]{3,2,1,0:T(8,128)S(1)}, u32[]{:S(2)}) copy-start(f32[2,24,24,256]{3,2,1,0:T(8,128)S(1)} %all-to-all-done.1.k_ref) | copy-start | bytes 3538948
  39.3 19.7 %all-to-all-start.2 = ((f32[32,8,640]{2,1,0:T(8,128)}), f32[32,8,640]{2,1,0:T(8,128)S(1)}, u32[]{:S(2)}, u32[]{:S(2)}) async-start(f32[32,8,640]{2,1,0:T(8,128)} %repack.2), calls=%async_computation.2 | async-start | bytes 1310720 | tf_op jit(solution)/shard_map/all_to_all | solution.py:354
  46.3 18.3 %collective-permute-start.3 = (f32[160,128]{1,0:T(8,128)S(1)}, f32[160,128]{1,0:T(8,128)S(1)}, u32[]{:S(2)}, u32[]{:S(2)}) collective-permute-start(f32[160,128]{1,0:T(8,128)S(1)} %slice_dynamic-update-slice_fusion), channel_id=1, source_target_pairs={{32,0},{64,32},{96,64},{128,96},{160,128},{192,160},{224,192},{256... | collective-permute-start | bytes 245768 | tf_op jit(solution)/shard_map/ppermute | solution.py:352
  47.6 17.0 %collective-permute-start.2 = (f32[160,128]{1,0:T(8,128)S(1)}, f32[160,128]{1,0:T(8,128)S(1)}, u32[]{:S(2)}, u32[]{:S(2)}) collective-permute-start(f32[160,128]{1,0:T(8,128)S(1)} %slice_dynamic-update-slice_fusion.2), channel_id=1, source_target_pairs={{0,32},{32,64},{64,96},{96,128},{128,160},{160,192},{192,224},{224... | collective-permute-start | bytes 245768 | tf_op jit(solution)/shard_map/ppermute | solution.py:351
  59.1 0.8 copy-start.1
  64.6 0.6 copy-start.3
  64.6 0.7 copy-start.4

commit v3 on v2

--- a/solution.py
+++ b/solution.py
@@ -118,7 +118,12 @@
     return jnp.sum(total, axis=0, keepdims=True)
 
 
-def conv_rows(mt_ref, k_ref, m_ref, s_ref):
+def by_core(kept, taken):
+    front = lax.axis_index("c") == 0
+    return jnp.concatenate([jnp.where(front, kept, taken), jnp.where(front, taken, kept)], axis=0)
+
+
+def conv_rows(mt_ref, kept_ref, taken_ref, m_ref, s_ref):
     core = lax.axis_index("c")
     lane = iota((8, 128), 1)
     m_ref[...] = jnp.zeros_like(m_ref)
@@ -141,8 +146,8 @@
     mh, ml = split(m_ref[...])
     per = 4
     for group in range(NB // per):
-        wide = jnp.concatenate(
-            [k_ref[s, per * group : per * group + per].reshape(per * NB, 256) for s in range(2)], axis=0
+        wide = by_core(
+            *(r[per * group : per * group + per].reshape(per * NB, 256) for r in (kept_ref, taken_ref))
         )
         p = product(wide, mh, ml)
         for i in range(per):
@@ -153,10 +158,12 @@
 
 def conv_edges(mh, ml, ks_ref, kn_ref, s_ref, out_ref):
     lane = iota((8, 128), 1)
-    wide = jnp.concatenate(
-        [jnp.concatenate([r[8 * HALO_TILES : 8 * HALO_TILES + 48], r[8 * HALO_TILES + 48 :]], axis=1) for r in (ks_ref, kn_ref)],
-        axis=0,
-    )
+    wide = []
+    for ref in (ks_ref, kn_ref):
+        at = 8 * HALO_TILES
+        rows = jnp.concatenate([ref[at : at + 48, :], ref[at + 48 : at + 96, :]], axis=1)
+        wide.append(by_core(rows[:NB], rows[NB:]))
+    wide = jnp.concatenate(wide, axis=0)
     p = product(wide, mh, ml)
     s_ref[0:1, :] = lagged(p[0:24], p[24:48])
     s_ref[25:26, :] = lagged(p[48:72], p[72:96])
@@ -178,13 +185,13 @@
         out_ref[lax.rem(base + k, 32)] = jnp.where(lane < 104, message, 0.0)
 
 
-def conv_kernel(mt_ref, k_ref, ks_ref, kn_ref, out_ref, m_ref, s_ref):
-    mh, ml = conv_rows(mt_ref, k_ref, m_ref, s_ref)
+def conv_kernel(mt_ref, kept_ref, taken_ref, ks_ref, kn_ref, out_ref, m_ref, s_ref):
+    mh, ml = conv_rows(mt_ref, kept_ref, taken_ref, m_ref, s_ref)
     conv_edges(mh, ml, ks_ref, kn_ref, s_ref, out_ref)
 
 
-def own_kernel(mt_ref, k_ref, rows_ref, mh_ref, ml_ref, m_ref, s_ref):
-    mh_ref[...], ml_ref[...] = conv_rows(mt_ref, k_ref, m_ref, s_ref)
+def own_kernel(mt_ref, kept_ref, taken_ref, rows_ref, mh_ref, ml_ref, m_ref, s_ref):
+    mh_ref[...], ml_ref[...] = conv_rows(mt_ref, kept_ref, taken_ref, m_ref, s_ref)
     rows_ref[...] = s_ref[1:25, :]
 
 
@@ -336,14 +343,16 @@
     from_east = lax.ppermute(to_west, LON, [((i + 1) % 32, i) for i in range(32)])
     column = lax.all_to_all(mass, ("zh", "zl"), 0, 0, tiled=True)
     turned = tied[0].transpose(0, 2, 1)
-    halves = jnp.stack([turned[:, :, :256], turned[:, :, 128:]])
-    column, from_west, from_east, halves = lax.optimization_barrier((column, from_west, from_east, halves))
-    k2 = lax.all_to_all(halves, "c", 0, 0, tiled=True)
-
+    front = lax.axis_index("c") == 0
+    kept = jnp.where(front, turned[:, :, :256], turned[:, :, 128:])
+    given = jnp.where(front, turned[:, :, 128:], turned[:, :, :256])
+    taken = lax.ppermute(given, "c", [(0, 1), (1, 0)])
+    column, from_west, from_east, kept, taken = lax.optimization_barrier(
+        (column, from_west, from_east, kept, taken)
+    )
     column = call(repack_kernel, "repack", struct(32, 8, 640), (column,))
-    column, k2 = lax.optimization_barrier((column, k2))
     def lat_message(rows, at, edge_row):
-        k = k2[:, edge_row].reshape(48, 256)
+        k = jnp.concatenate([kept[edge_row], taken[edge_row]], axis=0)
         return jnp.concatenate(
             [rows, from_east[at : at + 8], from_west[at : at + 8], k[:, :128], k[:, 128:]], axis=0
         )
@@ -354,7 +363,7 @@
     tiles = lax.all_to_all(column, ("y", "x", "c"), 0, 0, tiled=True)
     wide, coarse = pltpu.VMEM((256, 768), F32), pltpu.VMEM((32, 768), F32)
     half = jax.ShapeDtypeStruct((256, 768), BF16)
-    own = call(own_kernel, "own", (struct(NB, 768), half, half), (tiles, k2), (wide, coarse))
+    own = call(own_kernel, "own", (struct(NB, 768), half, half), (tiles, kept, taken), (wide, coarse))
     parts = call(edge_kernel, "edge", struct(32, 8, 128), (*own, from_south, from_north), (coarse,))
     parts = lax.all_to_all(parts, LON, 0, 0, tiled=True)
     *state, mass = call(
@@ -366,7 +375,7 @@
     column = lax.all_to_all(mass, ("zh", "zl"), 0, 0, tiled=True)
     column = call(repack_kernel, "repack", struct(32, 8, 640), (column,))
     tiles = lax.all_to_all(column, ("y", "x", "c"), 0, 0, tiled=True)
-    parts = call(conv_kernel, "conv", struct(32, 8, 128), (tiles, k2, from_south, from_north), (wide, coarse))
+    parts = call(conv_kernel, "conv", struct(32, 8, 128), (tiles, kept, taken, from_south, from_north), (wide, coarse))
     parts = lax.all_to_all(parts, LON, 0, 0, tiled=True)
     return call(
         last_kernel,

time: 158 us -> 154 us (0.975)
  blocking collectives: 75.8 us -> 72.1 us
  starting transfers between devices: 39.8 us -> 37.2 us
    ppermute x0 -> x1, starting transfers between devices: none -> 8.79 us  [body(): taken = lax.ppermute(given, 'c', [(0, 1), (1, 0)])]
    all_to_all x1, starting transfers between devices: 15.7 us -> 9.55 us  [body(): column = lax.all_to_all(mass, ('zh', 'zl'), 0, 0, tiled=True)]
    all_to_all x1 -> x0, starting transfers between devices: 6.13 us -> none  [body(): k2 = lax.all_to_all(halves, 'c', 0, 0, tiled=True)]
    all_to_all x1, blocking collectives: 28 us -> 24.3 us  [body(): column = lax.all_to_all(mass, ('zh', 'zl'), 0, 0, tiled=True)]
    all_to_all x1, starting transfers between devices: 6.82 us -> 9.09 us  [body(): tiles = lax.all_to_all(column, ('y', 'x', 'c'), 0, 0, tiled=True)]
  transfers between devices with their start and end apart: 7 -> 7, of which waited for: 2 -> 2; matrix products, arithmetic and copies ran while one was open for 1% -> 1% of each run, Pallas kernels for 6% -> 5%
where the time goes in v3:
time: 154 us; the launch traced here: 153 us
  blocking collectives  72.1 us (47%)
  starting transfers between devices  37.2 us (24%)
  Pallas kernels  26.9 us (17%)
  waiting for transfers between devices  11.9 us (8%)
  local copies, waits for them, and re-layouts  2.95 us (2%)
    all_to_all x2, blocking collectives, body(): parts = lax.all_to_all(parts, LON, 0, 0, tiled=True)  28.5 us
    pallas_call x9, Pallas kernels, call(): pl.pallas_call(kernel, name=name, out_shape=outs, in_specs=[VM] * len(ins...  26.9 us
    all_to_all x1, blocking collectives, body(): column = lax.all_to_all(mass, ('zh', 'zl'), 0, 0, tiled=True)  24.3 us
    all_to_all x1, blocking collectives, body(): tiles = lax.all_to_all(column, ('y', 'x', 'c'), 0, 0, tiled=True)  19.3 us
    all_to_all x1, starting transfers between devices, body(): column = lax.all_to_all(mass, ('zh', 'zl'), 0, 0, tiled=True)  9.55 us
    all_to_all x1, starting transfers between devices, body(): tiles = lax.all_to_all(column, ('y', 'x', 'c'), 0, 0, tiled=True)  9.09 us
    ppermute x1, starting transfers between devices, body(): taken = lax.ppermute(given, 'c', [(0, 1), (1, 0)])  8.79 us
    all_to_all x1, waiting for transfers between devices, body(): tiles = lax.all_to_all(column, ('y', 'x', 'c'), 0, 0, tiled=True)  8.17 us
  transfers between devices with their start and end apart: 7, of which 2 were waited for; matrix products, arithmetic and copies ran while one was open for 1% of the time, Pallas kernels for 5%

profile of v3, /device:TPU:1, one launch (start us, length us, event | category | flops | bytes accessed | tf_op | source)
XLA Modules:
  0.0 153.3 jit_solution(4499490652803155869)
XLA Ops:
  0.6 2.2 %mass.1 = f32[16,8,128]{2,1,0:T(8,128)} custom-call(f32[192,384]{1,0:T(8,128)} %h_ref.4, s32[192,384]{1,0:T(8,128)} %wet_ref.4), custom_call_target="tpu_custom_call" | custom-call | tf_op jit(solution)/shard_map/mass/pallas_call | solution.py:321
  2.9 1.3 slice_select_fusion
  4.2 8.8 %collective-permute-start.2 = (f32[24,24,256]{2,1,0:T(8,128)S(1)}, f32[24,24,256]{2,1,0:T(8,128)S(1)}, u32[]{:S(2)}, u32[]{:S(2)}) collective-permute-start(f32[24,24,256]{2,1,0:T(8,128)S(1)} %get-tuple-element.54), channel_id=1, source_target_pairs={{0,1},{1,0},{2,3},{3,2},{4,5},{5,4},{6,7},{7,6},{8,9},{9,8},{10,11... | collective-permute-start | bytes 1769480 | tf_op jit(solution)/shard_map/ppermute | solution.py:349
  13.0 9.6 %all-to-all-start = ((f32[16,8,128]{2,1,0:T(8,128)}), f32[16,8,128]{2,1,0:T(8,128)S(1)}, u32[]{:S(2)}, u32[]{:S(2)}) async-start(f32[16,8,128]{2,1,0:T(8,128)} %mass.1), calls=%async_computation | async-start | bytes 131072 | tf_op jit(solution)/shard_map/all_to_all | solution.py:344
  22.6 2.3 %pack.1 = (f32[192,128]{1,0:T(8,128)}, f32[192,128]{1,0:T(8,128)}, f32[48,128]{1,0:T(8,128)}, f32[48,128]{1,0:T(8,128)}) custom-call(f32[192,384]{1,0:T(8,128)} %h_ref.4, f32[192,384]{1,0:T(8,128)} %fl_ref.2, f32[192,384]{1,0:T(8,128)} %ft_ref.2, f32[192,384]{1,0:T(8,128)} %d_ref.2, s32[192,384]{1,0:T(8,128)} %wet_ref.4), custom_call_target="tpu_custom_call" | custom-call | tf_op jit(solution)/shard_map/pack/pallas_call | solution.py:321
  24.8 3.3 %collective-permute-start = (f32[192,128]{1,0:T(8,128)}, f32[192,128]{1,0:T(8,128)S(1)}, u32[]{:S(2)}, u32[]{:S(2)}) collective-permute-start(f32[192,128]{1,0:T(8,128)} %get-tuple-element.35), channel_id=1, source_target_pairs={{0,1},{1,2},{2,3},{3,4},{4,5},{5,6},{6,7},{7,8},{8,9},{9,10},{10,1... | collective-permute-start | bytes 294920 | tf_op jit(solution)/shard_map/ppermute | solution.py:342
  28.1 1.9 %collective-permute-start.1 = (f32[192,128]{1,0:T(8,128)}, f32[192,128]{1,0:T(8,128)S(1)}, u32[]{:S(2)}, u32[]{:S(2)}) collective-permute-start(f32[192,128]{1,0:T(8,128)} %get-tuple-element.36), channel_id=1, source_target_pairs={{1,0},{2,1},{3,2},{4,3},{5,4},{6,5},{7,6},{8,7},{9,8},{10,9},{11,1... | collective-permute-start | bytes 294920 | tf_op jit(solution)/shard_map/ppermute | solution.py:343
  30.0 0.8 constant_dynamic-update-slice_fusion.2
  30.8 0.0 collective-permute-done.fw_ref
  30.8 3.7 %collective-permute-done.1.fe_ref = f32[192,128]{1,0:T(8,128)S(1)} collective-permute-done((f32[192,128]{1,0:T(8,128)}, f32[192,128]{1,0:T(8,128)S(1)}, u32[]{:S(2)}, u32[]{:S(2)}) %collective-permute-start.1) | collective-permute-done | bytes 98336 | tf_op jit(solution)/shard_map/ppermute | solution.py:343
  34.6 0.0 all-to-all-done.in_ref
  34.6 0.6 copy-done.5
  35.2 1.8 %repack.2 = f32[32,8,640]{2,1,0:T(8,128)} custom-call(f32[16,8,128]{2,1,0:T(8,128)} %copy-done.5), custom_call_target="tpu_custom_call" | custom-call | tf_op jit(solution)/shard_map/repack/pallas_call | solution.py:321
  37.0 9.1 %all-to-all-start.1 = ((f32[32,8,640]{2,1,0:T(8,128)}), f32[32,8,640]{2,1,0:T(8,128)S(1)}, u32[]{:S(2)}, u32[]{:S(2)}) async-start(f32[32,8,640]{2,1,0:T(8,128)} %repack.2), calls=%async_computation.1 | async-start | bytes 1310720 | tf_op jit(solution)/shard_map/all_to_all | solution.py:363
  46.3 3.3 %collective-permute-start.3 = (f32[160,128]{1,0:T(8,128)S(1)}, f32[160,128]{1,0:T(8,128)S(1)}, u32[]{:S(2)}, u32[]{:S(2)}) collective-permute-start(f32[160,128]{1,0:T(8,128)S(1)} %fusion.5), channel_id=1, source_target_pairs={{0,32},{32,64},{64,96},{96,128},{128,160},{160,192},{192,224},{224... | collective-permute-start | bytes 245768 | tf_op jit(solution)/shard_map/ppermute | solution.py:360
  49.6 1.3 collective-permute-start.4
  50.9 8.2 %all-to-all-done.1.mt_ref = f32[32,8,640]{2,1,0:T(8,128)S(1)} async-done(((f32[32,8,640]{2,1,0:T(8,128)}), f32[32,8,640]{2,1,0:T(8,128)S(1)}, u32[]{:S(2)}, u32[]{:S(2)}) %all-to-all-start.1) | async-done | bytes 655392 | tf_op jit(solution)/shard_map/all_to_all | solution.py:363
  59.0 0.9 copy-done.1
  59.9 4.7 %own.1 = (f32[24,768]{1,0:T(8,128)}, bf16[256,768]{1,0:T(8,128)(2,1)}, bf16[256,768]{1,0:T(8,128)(2,1)}) custom-call(f32[32,8,640]{2,1,0:T(8,128)} %copy-done.1, f32[24,24,256]{2,1,0:T(8,128)} %copy-done, f32[24,24,256]{2,1,0:T(8,128)} %copy-done.2), custom_call_target="tpu_custom_call" | custom-call | tf_op jit(solution)/shard_map/own/pallas_call | solution.py:321
  64.6 0.0 collective-permute-done.3.ks_ref.fs_ref
  64.6 0.0 collective-permute-done.4.kn_ref.fn_ref
  64.6 0.6 copy-done.3
  65.2 0.0 copy-done.4
  65.3 2.5 %edge.1 = f32[32,8,128]{2,1,0:T(8,128)} custom-call(f32[24,768]{1,0:T(8,128)} %get-tuple-element.45.rows_ref, bf16[256,768]{1,0:T(8,128)(2,1)} %get-tuple-element.46.mh_ref, bf16[256,768]{1,0:T(8,128)(2,1)} %get-tuple-element.47.ml_ref, f32[160,128]{1,0:T(8,128)} %copy-done.3, f32[160,128]{1,0:T(8,128)} %copy-done.4), custom_call_target="tpu_custom_call" | custom-call | tf_op jit(solution)/shard_map/edge/pallas_call | solution.py:321
  67.7 15.1 %all_to_all.30.rs_ref = f32[32,8,128]{2,1,0:T(8,128)} all-to-all(f32[32,8,128]{2,1,0:T(8,128)} %edge.1), channel_id=1, replica_groups=mesh['zh'=4,'y'=4,'zl'=4,'x'=4,'c'=2] {'zl','x','c'}, dimensions={0} | all-to-all | bytes 262144 | tf_op jit(solution)/shard_map/all_to_all | solution.py:368
  82.8 3.7 %first.1 = (f32[200,512]{1,0:T(8,128)}, f32[200,512]{1,0:T(8,128)}, f32[200,512]{1,0:T(8,128)}, f32[200,512]{1,0:T(8,128)}, f32[200,512]{1,0:T(8,128)}, /*index=5*/f32[16,8,128]{2,1,0:T(8,128)}) custom-call(f32[192,384]{1,0:T(8,128)} %h_ref.4, f32[192,384]{1,0:T(8,128)} %fl_ref.2, f32[192,384]{1,0:T(8,128)} %ft_ref.2, f32[192,384]{1,0:T(8,128)} %d_ref.2, ...), custom_call_target="tpu_custom_call" | custom-call | tf_op jit(solution)/shard_map/first/pallas_call | solution.py:321
  86.5 24.3 %all_to_all.31.in_ref = f32[16,8,128]{2,1,0:T(8,128)} all-to-all(f32[16,8,128]{2,1,0:T(8,128)} %get-tuple-element.53), channel_id=1, replica_groups=mesh['zh'=4,'y'=4,'zl'=4,'x'=4,'c'=2] {'zh','zl'}, dimensions={0} | all-to-all | bytes 131072 | tf_op jit(solution)/shard_map/all_to_all | solution.py:375
  110.8 1.8 %repack.3 = f32[32,8,640]{2,1,0:T(8,128)} custom-call(f32[16,8,128]{2,1,0:T(8,128)} %all_to_all.31.in_ref), custom_call_target="tpu_custom_call" | custom-call | tf_op jit(solution)/shard_map/repack/pallas_call | solution.py:321
  112.6 19.3 %all_to_all.32.mt_ref = f32[32,8,640]{2,1,0:T(8,128)} all-to-all(f32[32,8,640]{2,1,0:T(8,128)} %repack.3), channel_id=1, replica_groups=mesh['zh'=4,'y'=4,'zl'=4,'x'=4,'c'=2] {'y','x','c'}, dimensions={0} | all-to-all | bytes 1310720 | tf_op jit(solution)/shard_map/all_to_all | solution.py:377
  131.9 5.0 %conv.1 = f32[32,8,128]{2,1,0:T(8,128)} custom-call(f32[32,8,640]{2,1,0:T(8,128)} %all_to_all.32.mt_ref, f32[24,24,256]{2,1,0:T(8,128)} %copy-done, f32[24,24,256]{2,1,0:T(8,128)} %copy-done.2, f32[160,128]{1,0:T(8,128)} %copy-done.3, f32[160,128]{1,0:T(8,128)} %copy-done.4), custom_call_target="tpu_custom_call" | custom-call | tf_op jit(solution)/shard_map/conv/pallas_call | solution.py:321
  136.9 13.4 %all_to_all.33.rs_ref = f32[32,8,128]{2,1,0:T(8,128)} all-to-all(f32[32,8,128]{2,1,0:T(8,128)} %conv.1), channel_id=1, replica_groups=mesh['zh'=4,'y'=4,'zl'=4,'x'=4,'c'=2] {'zl','x','c'}, dimensions={0} | all-to-all | bytes 262144 | tf_op jit(solution)/shard_map/all_to_all | solution.py:379
  150.3 3.0 %last.1 = (f32[192,384]{1,0:T(8,128)}, f32[192,384]{1,0:T(8,128)}, f32[192,384]{1,0:T(8,128)}, f32[24,24]{1,0:T(8,128)}) custom-call(f32[200,512]{1,0:T(8,128)} %get-tuple-element.48.h_ref, f32[200,512]{1,0:T(8,128)} %get-tuple-element.49.fl_ref, f32[200,512]{1,0:T(8,128)} %get-tuple-element.50.ft_ref, f32[200,512]{1,0:T(8,128)} %get-tuple-element.51.d_ref, ...), custom_call_target="tpu_custom_call" | custom-call | tf_op jit(solution)/shard_map/last/pallas_call | solution.py:321
  (20 shorter events, 0.1 us)
Async XLA Ops:
  4.2 41.9 %copy-start = (f32[24,24,256]{2,1,0:T(8,128)}, f32[24,24,256]{2,1,0:T(8,128)S(1)}, u32[]{:S(2)}) copy-start(f32[24,24,256]{2,1,0:T(8,128)S(1)} %get-tuple-element.41.kept_ref) | copy-start | bytes 1769476
  4.2 30.4 %collective-permute-start.2 = (f32[24,24,256]{2,1,0:T(8,128)S(1)}, f32[24,24,256]{2,1,0:T(8,128)S(1)}, u32[]{:S(2)}, u32[]{:S(2)}) collective-permute-start(f32[24,24,256]{2,1,0:T(8,128)S(1)} %get-tuple-element.54), channel_id=1, source_target_pairs={{0,1},{1,0},{2,3},{3,2},{4,5},{5,4},{6,7},{7,6},{8,9},{9,8},{10,11... | collective-permute-start | bytes 1769480 | tf_op jit(solution)/shard_map/ppermute | solution.py:349
  13.0 21.6 %all-to-all-start = ((f32[16,8,128]{2,1,0:T(8,128)}), f32[16,8,128]{2,1,0:T(8,128)S(1)}, u32[]{:S(2)}, u32[]{:S(2)}) async-start(f32[16,8,128]{2,1,0:T(8,128)} %mass.1), calls=%async_computation | async-start | bytes 131072 | tf_op jit(solution)/shard_map/all_to_all | solution.py:344
  24.8 6.0 %collective-permute-start = (f32[192,128]{1,0:T(8,128)}, f32[192,128]{1,0:T(8,128)S(1)}, u32[]{:S(2)}, u32[]{:S(2)}) collective-permute-start(f32[192,128]{1,0:T(8,128)} %get-tuple-element.35), channel_id=1, source_target_pairs={{0,1},{1,2},{2,3},{3,4},{4,5},{5,6},{6,7},{7,8},{8,9},{9,10},{10,1... | collective-permute-start | bytes 294920 | tf_op jit(solution)/shard_map/ppermute | solution.py:342
  28.1 6.4 %collective-permute-start.1 = (f32[192,128]{1,0:T(8,128)}, f32[192,128]{1,0:T(8,128)S(1)}, u32[]{:S(2)}, u32[]{:S(2)}) collective-permute-start(f32[192,128]{1,0:T(8,128)} %get-tuple-element.36), channel_id=1, source_target_pairs={{1,0},{2,1},{3,2},{4,3},{5,4},{6,5},{7,6},{8,7},{9,8},{10,9},{11,1... | collective-permute-start | bytes 294920 | tf_op jit(solution)/shard_map/ppermute | solution.py:343
  30.8 15.4 %copy-start.6 = (f32[192,128]{1,0:T(8,128)}, f32[192,128]{1,0:T(8,128)S(1)}, u32[]{:S(2)}) copy-start(f32[192,128]{1,0:T(8,128)S(1)} %collective-permute-done.fw_ref) | copy-start | bytes 294916
  34.6 11.6 %copy-start.7 = (f32[192,128]{1,0:T(8,128)}, f32[192,128]{1,0:T(8,128)S(1)}, u32[]{:S(2)}) copy-start(f32[192,128]{1,0:T(8,128)S(1)} %collective-permute-done.1.fe_ref) | copy-start | bytes 294916
  34.6 0.7 copy-start.5
  34.6 11.6 %copy-start.2 = (f32[24,24,256]{2,1,0:T(8,128)}, f32[24,24,256]{2,1,0:T(8,128)S(1)}, u32[]{:S(2)}) copy-start(f32[24,24,256]{2,1,0:T(8,128)S(1)} %collective-permute-done.2.taken_ref) | copy-start | bytes 1769476
  37.0 22.0 %all-to-all-start.1 = ((f32[32,8,640]{2,1,0:T(8,128)}), f32[32,8,640]{2,1,0:T(8,128)S(1)}, u32[]{:S(2)}, u32[]{:S(2)}) async-start(f32[32,8,640]{2,1,0:T(8,128)} %repack.2), calls=%async_computation.1 | async-start | bytes 1310720 | tf_op jit(solution)/shard_map/all_to_all | solution.py:363
  46.3 18.3 %collective-permute-start.3 = (f32[160,128]{1,0:T(8,128)S(1)}, f32[160,128]{1,0:T(8,128)S(1)}, u32[]{:S(2)}, u32[]{:S(2)}) collective-permute-start(f32[160,128]{1,0:T(8,128)S(1)} %fusion.5), channel_id=1, source_target_pairs={{0,32},{32,64},{64,96},{96,128},{128,160},{160,192},{192,224},{224... | collective-permute-start | bytes 245768 | tf_op jit(solution)/shard_map/ppermute | solution.py:360
  49.6 15.0 %collective-permute-start.4 = (f32[160,128]{1,0:T(8,128)S(1)}, f32[160,128]{1,0:T(8,128)S(1)}, u32[]{:S(2)}, u32[]{:S(2)}) collective-permute-start(f32[160,128]{1,0:T(8,128)S(1)} %fusion.4), channel_id=1, source_target_pairs={{32,0},{64,32},{96,64},{128,96},{160,128},{192,160},{224,192},{256... | collective-permute-start | bytes 245768 | tf_op jit(solution)/shard_map/ppermute | solution.py:361
  59.0 0.9 copy-start.1
  64.6 0.6 copy-start.3
  64.6 0.7 copy-start.4

commit v4 on v3

--- a/solution.py
+++ b/solution.py
@@ -116,6 +116,11 @@
         second, 24, 1, stride=1, stride_axis=0
     )
     return jnp.sum(total, axis=0, keepdims=True)
+
+
+def neighbours(outer, inner):
+    odd = lax.rem(lax.axis_index("y"), 2) == 1
+    return jnp.where(odd, inner, outer), jnp.where(odd, outer, inner)
 
 
 def by_core(kept, taken):
@@ -156,12 +161,12 @@
     return mh, ml
 
 
-def conv_edges(mh, ml, ks_ref, kn_ref, s_ref, out_ref):
+def conv_edges(mh, ml, outer_ref, inner_ref, s_ref, out_ref):
     lane = iota((8, 128), 1)
     wide = []
-    for ref in (ks_ref, kn_ref):
-        at = 8 * HALO_TILES
-        rows = jnp.concatenate([ref[at : at + 48, :], ref[at + 48 : at + 96, :]], axis=1)
+    at = 8 * HALO_TILES
+    for ref in neighbours(outer_ref[at : at + 96, :], inner_ref[at : at + 96, :]):
+        rows = jnp.concatenate([ref[:48], ref[48:]], axis=1)
         wide.append(by_core(rows[:NB], rows[NB:]))
     wide = jnp.concatenate(wide, axis=0)
     p = product(wide, mh, ml)
@@ -185,9 +190,9 @@
         out_ref[lax.rem(base + k, 32)] = jnp.where(lane < 104, message, 0.0)
 
 
-def conv_kernel(mt_ref, kept_ref, taken_ref, ks_ref, kn_ref, out_ref, m_ref, s_ref):
+def conv_kernel(mt_ref, kept_ref, taken_ref, inner_ref, outer_ref, out_ref, m_ref, s_ref):
     mh, ml = conv_rows(mt_ref, kept_ref, taken_ref, m_ref, s_ref)
-    conv_edges(mh, ml, ks_ref, kn_ref, s_ref, out_ref)
+    conv_edges(mh, ml, outer_ref, inner_ref, s_ref, out_ref)
 
 
 def own_kernel(mt_ref, kept_ref, taken_ref, rows_ref, mh_ref, ml_ref, m_ref, s_ref):
@@ -195,9 +200,9 @@
     rows_ref[...] = s_ref[1:25, :]
 
 
-def edge_kernel(rows_ref, mh_ref, ml_ref, ks_ref, kn_ref, out_ref, s_ref):
+def edge_kernel(rows_ref, mh_ref, ml_ref, inner_ref, outer_ref, out_ref, s_ref):
     s_ref[1:25, :] = rows_ref[...]
-    conv_edges(mh_ref[...], ml_ref[...], ks_ref, kn_ref, s_ref, out_ref)
+    conv_edges(mh_ref[...], ml_ref[...], outer_ref, inner_ref, s_ref, out_ref)
 
 
 def loading_tile(rs_ref):
@@ -262,7 +267,7 @@
 
 
 def first_kernel(
-    h_ref, fl_ref, ft_ref, d_ref, wet_ref, fe_ref, fw_ref, fs_ref, fn_ref, rs_ref,
+    h_ref, fl_ref, ft_ref, d_ref, wet_ref, fe_ref, fw_ref, inner_ref, outer_ref, rs_ref,
     h_out, fl_out, ft_out, d_out, w_out, mass_ref,
 ):
     lane = iota((ROWS, 128), 1)
@@ -276,17 +281,19 @@
             w = pltpu.roll(w, 2 * f, 1)
         return jnp.where(at < 2, e, jnp.where(at >= 126, w, 0.0))
 
+    south, north = neighbours(outer_ref[:64, :], inner_ref[:64, :])
+
     def edge(ref, f, first):
         at = 0 if f < 4 else 24
-        tiles = [ref[at + 8 * t : at + 8 * t + 8, :] for t in range(3)]
+        tiles = [ref[at + 8 * t : at + 8 * t + 8] for t in range(3)]
         shift = (first - 2 * f) % 8 if f < 4 else 0
         tiles = [pltpu.roll(x, shift, 0) for x in tiles] if shift else tiles
-        return tiles + [side(ref[48:56, :], ref[56:64, :], f, lane8)]
+        return tiles + [side(ref[48:56], ref[56:64], f, lane8)]
 
     ext = []
     for f, x in enumerate((h_ref[...], fl_ref[...], ft_ref[...], d_ref[...], wet_ref[...].astype(F32))):
         main = jnp.concatenate([x, side(fe_ref[...], fw_ref[...], f, lane)], axis=1)
-        from_south, from_north = edge(fs_ref, f, 6), edge(fn_ref, f, 0)
+        from_south, from_north = edge(south, f, 6), edge(north, f, 0)
         tail = jnp.concatenate(
             [jnp.where(sub8 < 4, n, s) for n, s in zip(from_north, from_south)], axis=1
         )
@@ -357,25 +364,28 @@
             [rows, from_east[at : at + 8], from_west[at : at + 8], k[:, :128], k[:, 128:]], axis=0
         )
 
-    from_south = lax.ppermute(lat_message(to_north, ROWS - 8, 23), LAT, [(i, i + 1) for i in range(15)])
-    from_north = lax.ppermute(lat_message(to_south, 0, 0), LAT, [(i + 1, i) for i in range(15)])
-
+    odd = lax.rem(lax.axis_index("y"), 2) == 1
+    up, down = lat_message(to_north, ROWS - 8, 23), lat_message(to_south, 0, 0)
+    outer = [(i + a, i + 1 - a) for i in range(1, 15, 2) for a in range(2)]
+    inner = [(i + a, i + 1 - a) for i in range(0, 16, 2) for a in range(2)]
+    inner = lax.ppermute(jnp.where(odd, down, up), LAT, inner)
+    outer = lax.ppermute(jnp.where(odd, up, down), LAT, outer)
     tiles = lax.all_to_all(column, ("y", "x", "c"), 0, 0, tiled=True)
     wide, coarse = pltpu.VMEM((256, 768), F32), pltpu.VMEM((32, 768), F32)
     half = jax.ShapeDtypeStruct((256, 768), BF16)
     own = call(own_kernel, "own", (struct(NB, 768), half, half), (tiles, kept, taken), (wide, coarse))
-    parts = call(edge_kernel, "edge", struct(32, 8, 128), (*own, from_south, from_north), (coarse,))
+    parts = call(edge_kernel, "edge", struct(32, 8, 128), (*own, inner, outer), (coarse,))
     parts = lax.all_to_all(parts, LON, 0, 0, tiled=True)
     *state, mass = call(
         first_kernel,
         "first",
         (struct(EROWS, ECOLS),) * 5 + (struct(16, 8, 128),),
-        fields + (from_east, from_west, from_south, from_north, parts),
+        fields + (from_east, from_west, inner, outer, parts),
     )
     column = lax.all_to_all(mass, ("zh", "zl"), 0, 0, tiled=True)
     column = call(repack_kernel, "repack", struct(32, 8, 640), (column,))
     tiles = lax.all_to_all(column, ("y", "x", "c"), 0, 0, tiled=True)
-    parts = call(conv_kernel, "conv", struct(32, 8, 128), (tiles, kept, taken, from_south, from_north), (wide, coarse))
+    parts = call(conv_kernel, "conv", struct(32, 8, 128), (tiles, kept, taken, inner, outer), (wide, coarse))
     parts = lax.all_to_all(parts, LON, 0, 0, tiled=True)
     return call(
         last_kernel,

time: 154 us -> 154 us (level)
  starting transfers between devices: 37.2 us -> 39.2 us
  waiting for transfers between devices: 11.9 us -> 10.1 us
    all_to_all x1, waiting for transfers between devices: 8.17 us -> 6.34 us  [body(): tiles = lax.all_to_all(column, ('y', 'x', 'c'), 0, 0, tiled=True)]
    ppermute x2, starting transfers between devices: 4.59 us -> 6.39 us  [the longest x1 5.73 us: body(): inner = lax.ppermute(jnp.where(odd, down, up), LAT, inner)]
where the time goes in v4:
time: 154 us; the launch traced here: 153 us
  blocking collectives  71.5 us (46%)
  starting transfers between devices  39.2 us (25%)
  Pallas kernels  27 us (18%)
  waiting for transfers between devices  10.1 us (7%)
  local copies, waits for them, and re-layouts  2.93 us (2%)
    all_to_all x2, blocking collectives, body(): parts = lax.all_to_all(parts, LON, 0, 0, tiled=True)  28.4 us
    pallas_call x9, Pallas kernels, call(): pl.pallas_call(kernel, name=name, out_shape=outs, in_specs=[VM] * len(ins...  27 us
    all_to_all x1, blocking collectives, body(): column = lax.all_to_all(mass, ('zh', 'zl'), 0, 0, tiled=True)  23.8 us
    all_to_all x1, blocking collectives, body(): tiles = lax.all_to_all(column, ('y', 'x', 'c'), 0, 0, tiled=True)  19.3 us
    all_to_all x1, starting transfers between devices, body(): column = lax.all_to_all(mass, ('zh', 'zl'), 0, 0, tiled=True)  9.55 us
    all_to_all x1, starting transfers between devices, body(): tiles = lax.all_to_all(column, ('y', 'x', 'c'), 0, 0, tiled=True)  9.09 us
    ppermute x1, starting transfers between devices, body(): taken = lax.ppermute(given, 'c', [(0, 1), (1, 0)])  8.79 us
    all_to_all x1, waiting for transfers between devices, body(): tiles = lax.all_to_all(column, ('y', 'x', 'c'), 0, 0, tiled=True)  6.34 us
  transfers between devices with their start and end apart: 7, of which 2 were waited for; matrix products, arithmetic and copies ran while one was open for 1% of the time, Pallas kernels for 5%

profile of v4, /device:TPU:1, one launch (start us, length us, event | category | flops | bytes accessed | tf_op | source)
XLA Modules:
  0.0 152.8 jit_solution(8042342101970645256)
XLA Ops:
  0.6 2.2 %mass.1 = f32[16,8,128]{2,1,0:T(8,128)} custom-call(f32[192,384]{1,0:T(8,128)} %h_ref.4, s32[192,384]{1,0:T(8,128)} %wet_ref.4), custom_call_target="tpu_custom_call" | custom-call | tf_op jit(solution)/shard_map/mass/pallas_call | solution.py:328
  2.9 1.3 slice_select_fusion
  4.2 8.8 %collective-permute-start.2 = (f32[24,24,256]{2,1,0:T(8,128)S(1)}, f32[24,24,256]{2,1,0:T(8,128)S(1)}, u32[]{:S(2)}, u32[]{:S(2)}) collective-permute-start(f32[24,24,256]{2,1,0:T(8,128)S(1)} %get-tuple-element.54), channel_id=1, source_target_pairs={{0,1},{1,0},{2,3},{3,2},{4,5},{5,4},{6,7},{7,6},{8,9},{9,8},{10,11... | collective-permute-start | bytes 1769480 | tf_op jit(solution)/shard_map/ppermute | solution.py:356
  13.0 9.6 %all-to-all-start = ((f32[16,8,128]{2,1,0:T(8,128)}), f32[16,8,128]{2,1,0:T(8,128)S(1)}, u32[]{:S(2)}, u32[]{:S(2)}) async-start(f32[16,8,128]{2,1,0:T(8,128)} %mass.1), calls=%async_computation | async-start | bytes 131072 | tf_op jit(solution)/shard_map/all_to_all | solution.py:351
  22.6 2.3 %pack.1 = (f32[192,128]{1,0:T(8,128)}, f32[192,128]{1,0:T(8,128)}, f32[48,128]{1,0:T(8,128)}, f32[48,128]{1,0:T(8,128)}) custom-call(f32[192,384]{1,0:T(8,128)} %h_ref.4, f32[192,384]{1,0:T(8,128)} %fl_ref.2, f32[192,384]{1,0:T(8,128)} %ft_ref.2, f32[192,384]{1,0:T(8,128)} %d_ref.2, s32[192,384]{1,0:T(8,128)} %wet_ref.4), custom_call_target="tpu_custom_call" | custom-call | tf_op jit(solution)/shard_map/pack/pallas_call | solution.py:328
  24.8 3.4 %collective-permute-start = (f32[192,128]{1,0:T(8,128)}, f32[192,128]{1,0:T(8,128)S(1)}, u32[]{:S(2)}, u32[]{:S(2)}) collective-permute-start(f32[192,128]{1,0:T(8,128)} %get-tuple-element.35), channel_id=1, source_target_pairs={{0,1},{1,2},{2,3},{3,4},{4,5},{5,6},{6,7},{7,8},{8,9},{9,10},{10,1... | collective-permute-start | bytes 294920 | tf_op jit(solution)/shard_map/ppermute | solution.py:349
  28.3 1.9 %collective-permute-start.1 = (f32[192,128]{1,0:T(8,128)}, f32[192,128]{1,0:T(8,128)S(1)}, u32[]{:S(2)}, u32[]{:S(2)}) collective-permute-start(f32[192,128]{1,0:T(8,128)} %get-tuple-element.36), channel_id=1, source_target_pairs={{1,0},{2,1},{3,2},{4,3},{5,4},{6,5},{7,6},{8,7},{9,8},{10,9},{11,1... | collective-permute-start | bytes 294920 | tf_op jit(solution)/shard_map/ppermute | solution.py:350
  30.2 0.7 constant_dynamic-update-slice_fusion.2
  30.9 0.0 collective-permute-done.fw_ref
  30.9 3.7 %collective-permute-done.1.fe_ref = f32[192,128]{1,0:T(8,128)S(1)} collective-permute-done((f32[192,128]{1,0:T(8,128)}, f32[192,128]{1,0:T(8,128)S(1)}, u32[]{:S(2)}, u32[]{:S(2)}) %collective-permute-start.1) | collective-permute-done | bytes 98336 | tf_op jit(solution)/shard_map/ppermute | solution.py:350
  34.7 0.0 all-to-all-done.in_ref
  34.7 0.0 collective-permute-done.2.taken_ref
  34.7 0.6 copy-done.5
  35.4 1.8 %repack.2 = f32[32,8,640]{2,1,0:T(8,128)} custom-call(f32[16,8,128]{2,1,0:T(8,128)} %copy-done.5), custom_call_target="tpu_custom_call" | custom-call | tf_op jit(solution)/shard_map/repack/pallas_call | solution.py:328
  37.2 9.1 %all-to-all-start.1 = ((f32[32,8,640]{2,1,0:T(8,128)}), f32[32,8,640]{2,1,0:T(8,128)S(1)}, u32[]{:S(2)}, u32[]{:S(2)}) async-start(f32[32,8,640]{2,1,0:T(8,128)} %repack.2), calls=%async_computation.1 | async-start | bytes 1310720 | tf_op jit(solution)/shard_map/all_to_all | solution.py:373
  46.4 0.7 collective-permute-start.4
  47.1 5.7 %collective-permute-start.3 = (f32[160,128]{1,0:T(8,128)S(1)}, f32[160,128]{1,0:T(8,128)S(1)}, u32[]{:S(2)}, u32[]{:S(2)}) collective-permute-start(f32[160,128]{1,0:T(8,128)S(1)} %get-tuple-element.61), channel_id=1, source_target_pairs={{0,32},{32,0},{64,96},{96,64},{128,160},{160,128},{192,224},{224,1... | collective-permute-start | bytes 245768 | tf_op jit(solution)/shard_map/ppermute | solution.py:371
  52.8 6.3 %all-to-all-done.1.mt_ref = f32[32,8,640]{2,1,0:T(8,128)S(1)} async-done(((f32[32,8,640]{2,1,0:T(8,128)}), f32[32,8,640]{2,1,0:T(8,128)S(1)}, u32[]{:S(2)}, u32[]{:S(2)}) %all-to-all-start.1) | async-done | bytes 655392 | tf_op jit(solution)/shard_map/all_to_all | solution.py:373
  59.2 0.9 copy-done.1
  60.0 4.7 %own.1 = (f32[24,768]{1,0:T(8,128)}, bf16[256,768]{1,0:T(8,128)(2,1)}, bf16[256,768]{1,0:T(8,128)(2,1)}) custom-call(f32[32,8,640]{2,1,0:T(8,128)} %copy-done.1, f32[24,24,256]{2,1,0:T(8,128)} %copy-done, f32[24,24,256]{2,1,0:T(8,128)} %copy-done.2), custom_call_target="tpu_custom_call" | custom-call | tf_op jit(solution)/shard_map/own/pallas_call | solution.py:328
  64.7 0.0 collective-permute-done.3.inner_ref
  64.7 0.6 copy-done.3
  65.4 0.0 copy-done.4
  65.4 2.5 %edge.1 = f32[32,8,128]{2,1,0:T(8,128)} custom-call(f32[24,768]{1,0:T(8,128)} %get-tuple-element.45.rows_ref, bf16[256,768]{1,0:T(8,128)(2,1)} %get-tuple-element.46.mh_ref, bf16[256,768]{1,0:T(8,128)(2,1)} %get-tuple-element.47.ml_ref, f32[160,128]{1,0:T(8,128)} %copy-done.4, f32[160,128]{1,0:T(8,128)} %copy-done.3), custom_call_target="tpu_custom_call" | custom-call | tf_op jit(solution)/shard_map/edge/pallas_call | solution.py:328
  67.8 15.0 %all_to_all.30.rs_ref = f32[32,8,128]{2,1,0:T(8,128)} all-to-all(f32[32,8,128]{2,1,0:T(8,128)} %edge.1), channel_id=1, replica_groups=mesh['zh'=4,'y'=4,'zl'=4,'x'=4,'c'=2] {'zl','x','c'}, dimensions={0} | all-to-all | bytes 262144 | tf_op jit(solution)/shard_map/all_to_all | solution.py:378
  82.8 3.7 %first.1 = (f32[200,512]{1,0:T(8,128)}, f32[200,512]{1,0:T(8,128)}, f32[200,512]{1,0:T(8,128)}, f32[200,512]{1,0:T(8,128)}, f32[200,512]{1,0:T(8,128)}, /*index=5*/f32[16,8,128]{2,1,0:T(8,128)}) custom-call(f32[192,384]{1,0:T(8,128)} %h_ref.4, f32[192,384]{1,0:T(8,128)} %fl_ref.2, f32[192,384]{1,0:T(8,128)} %ft_ref.2, f32[192,384]{1,0:T(8,128)} %d_ref.2, ...), custom_call_target="tpu_custom_call" | custom-call | tf_op jit(solution)/shard_map/first/pallas_call | solution.py:328
  86.5 23.8 %all_to_all.31.in_ref = f32[16,8,128]{2,1,0:T(8,128)} all-to-all(f32[16,8,128]{2,1,0:T(8,128)} %get-tuple-element.53), channel_id=1, replica_groups=mesh['zh'=4,'y'=4,'zl'=4,'x'=4,'c'=2] {'zh','zl'}, dimensions={0} | all-to-all | bytes 131072 | tf_op jit(solution)/shard_map/all_to_all | solution.py:385
  110.4 1.8 %repack.3 = f32[32,8,640]{2,1,0:T(8,128)} custom-call(f32[16,8,128]{2,1,0:T(8,128)} %all_to_all.31.in_ref), custom_call_target="tpu_custom_call" | custom-call | tf_op jit(solution)/shard_map/repack/pallas_call | solution.py:328
  112.2 19.3 %all_to_all.32.mt_ref = f32[32,8,640]{2,1,0:T(8,128)} all-to-all(f32[32,8,640]{2,1,0:T(8,128)} %repack.3), channel_id=1, replica_groups=mesh['zh'=4,'y'=4,'zl'=4,'x'=4,'c'=2] {'y','x','c'}, dimensions={0} | all-to-all | bytes 1310720 | tf_op jit(solution)/shard_map/all_to_all | solution.py:387
  131.5 5.0 %conv.1 = f32[32,8,128]{2,1,0:T(8,128)} custom-call(f32[32,8,640]{2,1,0:T(8,128)} %all_to_all.32.mt_ref, f32[24,24,256]{2,1,0:T(8,128)} %copy-done, f32[24,24,256]{2,1,0:T(8,128)} %copy-done.2, f32[160,128]{1,0:T(8,128)} %copy-done.4, f32[160,128]{1,0:T(8,128)} %copy-done.3), custom_call_target="tpu_custom_call" | custom-call | tf_op jit(solution)/shard_map/conv/pallas_call | solution.py:328
  136.5 13.4 %all_to_all.33.rs_ref = f32[32,8,128]{2,1,0:T(8,128)} all-to-all(f32[32,8,128]{2,1,0:T(8,128)} %conv.1), channel_id=1, replica_groups=mesh['zh'=4,'y'=4,'zl'=4,'x'=4,'c'=2] {'zl','x','c'}, dimensions={0} | all-to-all | bytes 262144 | tf_op jit(solution)/shard_map/all_to_all | solution.py:389
  149.9 3.0 %last.1 = (f32[192,384]{1,0:T(8,128)}, f32[192,384]{1,0:T(8,128)}, f32[192,384]{1,0:T(8,128)}, f32[24,24]{1,0:T(8,128)}) custom-call(f32[200,512]{1,0:T(8,128)} %get-tuple-element.48.h_ref, f32[200,512]{1,0:T(8,128)} %get-tuple-element.49.fl_ref, f32[200,512]{1,0:T(8,128)} %get-tuple-element.50.ft_ref, f32[200,512]{1,0:T(8,128)} %get-tuple-element.51.d_ref, ...), custom_call_target="tpu_custom_call" | custom-call | tf_op jit(solution)/shard_map/last/pallas_call | solution.py:328
  (23 shorter events, 0.1 us)
Async XLA Ops:
  4.2 42.1 %copy-start = (f32[24,24,256]{2,1,0:T(8,128)}, f32[24,24,256]{2,1,0:T(8,128)S(1)}, u32[]{:S(2)}) copy-start(f32[24,24,256]{2,1,0:T(8,128)S(1)} %get-tuple-element.41.kept_ref) | copy-start | bytes 1769476
  4.2 30.5 %collective-permute-start.2 = (f32[24,24,256]{2,1,0:T(8,128)S(1)}, f32[24,24,256]{2,1,0:T(8,128)S(1)}, u32[]{:S(2)}, u32[]{:S(2)}) collective-permute-start(f32[24,24,256]{2,1,0:T(8,128)S(1)} %get-tuple-element.54), channel_id=1, source_target_pairs={{0,1},{1,0},{2,3},{3,2},{4,5},{5,4},{6,7},{7,6},{8,9},{9,8},{10,11... | collective-permute-start | bytes 1769480 | tf_op jit(solution)/shard_map/ppermute | solution.py:356
  13.0 21.7 %all-to-all-start = ((f32[16,8,128]{2,1,0:T(8,128)}), f32[16,8,128]{2,1,0:T(8,128)S(1)}, u32[]{:S(2)}, u32[]{:S(2)}) async-start(f32[16,8,128]{2,1,0:T(8,128)} %mass.1), calls=%async_computation | async-start | bytes 131072 | tf_op jit(solution)/shard_map/all_to_all | solution.py:351
  24.8 5.4 %copy-start.8 = (f32[48,128]{1,0:T(8,128)S(1)}, f32[48,128]{1,0:T(8,128)}, u32[]{:S(2)}) copy-start(f32[48,128]{1,0:T(8,128)} %get-tuple-element.43) | copy-start | bytes 73732
  24.8 6.1 %collective-permute-start = (f32[192,128]{1,0:T(8,128)}, f32[192,128]{1,0:T(8,128)S(1)}, u32[]{:S(2)}, u32[]{:S(2)}) collective-permute-start(f32[192,128]{1,0:T(8,128)} %get-tuple-element.35), channel_id=1, source_target_pairs={{0,1},{1,2},{2,3},{3,4},{4,5},{5,6},{6,7},{7,8},{8,9},{9,10},{10,1... | collective-permute-start | bytes 294920 | tf_op jit(solution)/shard_map/ppermute | solution.py:349
  28.3 6.4 %collective-permute-start.1 = (f32[192,128]{1,0:T(8,128)}, f32[192,128]{1,0:T(8,128)S(1)}, u32[]{:S(2)}, u32[]{:S(2)}) collective-permute-start(f32[192,128]{1,0:T(8,128)} %get-tuple-element.36), channel_id=1, source_target_pairs={{1,0},{2,1},{3,2},{4,3},{5,4},{6,5},{7,6},{8,7},{9,8},{10,9},{11,1... | collective-permute-start | bytes 294920 | tf_op jit(solution)/shard_map/ppermute | solution.py:350
  30.9 15.4 %copy-start.6 = (f32[192,128]{1,0:T(8,128)}, f32[192,128]{1,0:T(8,128)S(1)}, u32[]{:S(2)}) copy-start(f32[192,128]{1,0:T(8,128)S(1)} %collective-permute-done.fw_ref) | copy-start | bytes 294916
  34.7 11.6 %copy-start.7 = (f32[192,128]{1,0:T(8,128)}, f32[192,128]{1,0:T(8,128)S(1)}, u32[]{:S(2)}) copy-start(f32[192,128]{1,0:T(8,128)S(1)} %collective-permute-done.1.fe_ref) | copy-start | bytes 294916
  34.7 0.7 copy-start.5
  34.7 11.6 %copy-start.2 = (f32[24,24,256]{2,1,0:T(8,128)}, f32[24,24,256]{2,1,0:T(8,128)S(1)}, u32[]{:S(2)}) copy-start(f32[24,24,256]{2,1,0:T(8,128)S(1)} %collective-permute-done.2.taken_ref) | copy-start | bytes 1769476
  37.2 22.0 %all-to-all-start.1 = ((f32[32,8,640]{2,1,0:T(8,128)}), f32[32,8,640]{2,1,0:T(8,128)S(1)}, u32[]{:S(2)}, u32[]{:S(2)}) async-start(f32[32,8,640]{2,1,0:T(8,128)} %repack.2), calls=%async_computation.1 | async-start | bytes 1310720 | tf_op jit(solution)/shard_map/all_to_all | solution.py:373
  46.4 18.3 %collective-permute-start.4 = (f32[160,128]{1,0:T(8,128)S(1)}, f32[160,128]{1,0:T(8,128)S(1)}, u32[]{:S(2)}, u32[]{:S(2)}) collective-permute-start(f32[160,128]{1,0:T(8,128)S(1)} %get-tuple-element.60), channel_id=1, source_target_pairs={{32,64},{64,32},{96,128},{128,96},{160,192},{192,160},{224,256},{2... | collective-permute-start | bytes 245768 | tf_op jit(solution)/shard_map/ppermute | solution.py:372
  47.1 17.6 %collective-permute-start.3 = (f32[160,128]{1,0:T(8,128)S(1)}, f32[160,128]{1,0:T(8,128)S(1)}, u32[]{:S(2)}, u32[]{:S(2)}) collective-permute-start(f32[160,128]{1,0:T(8,128)S(1)} %get-tuple-element.61), channel_id=1, source_target_pairs={{0,32},{32,0},{64,96},{96,64},{128,160},{160,128},{192,224},{224,1... | collective-permute-start | bytes 245768 | tf_op jit(solution)/shard_map/ppermute | solution.py:371
  59.2 0.9 copy-start.1
  64.7 0.6 copy-start.3
  64.7 0.7 copy-start.4
